TPU v7x, 128 devices: a whole 4x4x4 slice. The times are simulated.
128 devices in a mesh: bank: 8 (over z, core), freq: 16 (over y, x).
Axes of the slice: x: 4, y: 4, z: 4, core: 2. Of those that a mesh axis runs over, the one named last changes fastest.
Arguments:
- strain: float32 [3, 2, 512, 2048], P(None, None, 'freq', 'bank'), may hold values from -6 to 6
- templates: float32 [16, 2, 512, 2048], P('bank', None, 'freq'), may hold values from -6 to 6
- coinc_tmpl: int32 [8], P('bank'), may hold values from 0 to 1
- coinc_det: int32 [8], P('bank'), may hold values from 0 to 2
- bin_edges: int32 [16, 15], P('bank'), may hold values from 1 to 31, as said below
Outputs:
- snr: float32 [16, 3, 2, 2048, 512], P('bank', None, None, 'freq')
- chi_sq: float32 [8, 2048, 512], P('bank', 'freq')
Inputs may be any that keep to these rules, and one draw needn't show every extreme that they name: `coinc_tmpl`: the entries of shard j // 1 of bank name templates of that shard. `bin_edges`: each row is strictly increasing.
All inputs are finite; a program needn't handle non-finite values.
Results may differ from a plain program's by a relative error of at most 0.0003.
Values sent between devices are 32-bit elements; how exact they have to be, the bound alone decides.
A program may use at most 128 MiB of HBM per device.

v0:
```python
import math

import jax
import jax.numpy as jnp
from jax import lax
from jax.sharding import PartitionSpec as P

N1 = 2048
N2 = 512
NBLK = 32
BINS = 16


def phase(row_index, col_index, length):
    product = row_index[:, None] * col_index[None, :] % length
    angle = product.astype(jnp.float32) * (2.0 * math.pi / length)
    return (jnp.cos(angle), jnp.sin(angle))


def per_device(strain, templates, coinc_tmpl, coinc_det, bin_edges):
    highest = lax.Precision.HIGHEST
    strain_all = lax.all_gather(strain, "bank", axis=3, tiled=True)
    strain_re = strain_all[:, 0]
    strain_im = strain_all[:, 1]
    tmpl_re = templates[:, 0]
    tmpl_im = templates[:, 1]
    tmpl_count, col_count, row_total = tmpl_re.shape
    det_count = strain_re.shape[0]
    prod_re = tmpl_re[:, None] * strain_re[None] + tmpl_im[:, None] * strain_im[None]
    prod_im = tmpl_re[:, None] * strain_im[None] - tmpl_im[:, None] * strain_re[None]
    block_rows = N1 // NBLK
    local_power = (
        (tmpl_re * tmpl_re + tmpl_im * tmpl_im)
        .reshape(tmpl_count, col_count, NBLK, block_rows)
        .sum(axis=(1, 3))
    )
    block_power = lax.psum(local_power, "freq")
    sigma_sq = block_power.sum(axis=1)
    inv_sigma = lax.rsqrt(sigma_sq)
    row_index = jnp.arange(N1, dtype=jnp.int32)
    first_cos, first_sin = phase(row_index, row_index, N1)
    form = "tdck,kn->tdcn"
    section_re = jnp.einsum(form, prod_re, first_cos, precision=highest) - jnp.einsum(
        form, prod_im, first_sin, precision=highest
    )
    section_im = jnp.einsum(form, prod_re, first_sin, precision=highest) + jnp.einsum(
        form, prod_im, first_cos, precision=highest
    )
    col_global = lax.axis_index("freq") * col_count + jnp.arange(col_count, dtype=jnp.int32)
    twist_cos, twist_sin = phase(col_global, row_index, N1 * N2)
    scaling = inv_sigma[:, None, None, None]
    whole_re = (section_re * twist_cos - section_im * twist_sin) * scaling
    whole_im = (section_re * twist_sin + section_im * twist_cos) * scaling
    bin_of = jnp.sum(
        jnp.arange(NBLK, dtype=jnp.int32)[None, :, None] >= bin_edges[:, None, :], axis=2
    )
    bin_mask = (bin_of[:, :, None] == jnp.arange(BINS, dtype=jnp.int32)[None, None, :]).astype(
        jnp.float32
    )
    weights = jnp.einsum("tb,tbl->tl", block_power, bin_mask, precision=highest) / sigma_sq[:, None]
    pick_tmpl = (coinc_tmpl[:, None] == jnp.arange(tmpl_count, dtype=jnp.int32)[None, :]).astype(
        jnp.float32
    )
    pick_det = (coinc_det[:, None] == jnp.arange(det_count, dtype=jnp.int32)[None, :]).astype(
        jnp.float32
    )
    picked = pick_tmpl[:, :, None] * pick_det[:, None, :]
    entry_re = jnp.einsum("jtd,tdck->jck", picked, prod_re, precision=highest)
    entry_im = jnp.einsum("jtd,tdck->jck", picked, prod_im, precision=highest)
    slot_count = entry_re.shape[0]
    entry_re = entry_re.reshape(slot_count, col_count, NBLK, block_rows)
    entry_im = entry_im.reshape(slot_count, col_count, NBLK, block_rows)
    block_cos = first_cos.reshape(NBLK, block_rows, N1)
    block_sin = first_sin.reshape(NBLK, block_rows, N1)
    form_block = "jcbk,bkn->jbcn"
    block_re = jnp.einsum(form_block, entry_re, block_cos, precision=highest) - jnp.einsum(
        form_block, entry_im, block_sin, precision=highest
    )
    block_im = jnp.einsum(form_block, entry_re, block_sin, precision=highest) + jnp.einsum(
        form_block, entry_im, block_cos, precision=highest
    )
    slot_bins = jnp.einsum("jt,tbl->jbl", pick_tmpl, bin_mask, precision=highest)
    slot_inv = jnp.einsum("jt,t->j", pick_tmpl, inv_sigma, precision=highest)
    slot_weights = jnp.einsum("jt,tl->jl", pick_tmpl, weights, precision=highest)
    raw_re = jnp.einsum("jbcn,jbl->jlcn", block_re, slot_bins, precision=highest)
    raw_im = jnp.einsum("jbcn,jbl->jlcn", block_im, slot_bins, precision=highest)
    slot_scale = slot_inv[:, None, None, None]
    bins_re = (raw_re * twist_cos - raw_im * twist_sin) * slot_scale
    bins_im = (raw_re * twist_sin + raw_im * twist_cos) * slot_scale
    col_index = jnp.arange(N2, dtype=jnp.int32)
    second_cos, second_sin = phase(col_index, col_index, N2)

    def section_two(pieces):
        part_re, part_im = pieces
        form_two = "...cn,cm->...nm"
        out_re = jnp.einsum(form_two, part_re, second_cos, precision=highest) - jnp.einsum(
            form_two, part_im, second_sin, precision=highest
        )
        out_im = jnp.einsum(form_two, part_re, second_sin, precision=highest) + jnp.einsum(
            form_two, part_im, second_cos, precision=highest
        )
        return (out_re, out_im)

    out_re, out_im = section_two(
        (
            lax.all_to_all(whole_re, "freq", split_axis=3, concat_axis=2, tiled=True),
            lax.all_to_all(whole_im, "freq", split_axis=3, concat_axis=2, tiled=True),
        )
    )
    snr = jnp.stack([out_re, out_im], 2)
    level_re, level_im = section_two(
        (
            lax.all_to_all(bins_re, "freq", split_axis=3, concat_axis=2, tiled=True),
            lax.all_to_all(bins_im, "freq", split_axis=3, concat_axis=2, tiled=True),
        )
    )
    total_re = level_re.sum(axis=1)
    total_im = level_im.sum(axis=1)
    spread = slot_weights[:, :, None, None]
    dev_re = level_re - spread * total_re[:, None]
    dev_im = level_im - spread * total_im[:, None]
    chi_sq = jnp.sum((dev_re * dev_re + dev_im * dev_im) / spread, axis=1)
    return (snr, chi_sq)


def solution(mesh):
    placed = (
        P(None, None, "freq", "bank"),
        P("bank", None, "freq", None),
        P("bank"),
        P("bank"),
        P("bank", None),
    )
    return jax.shard_map(
        per_device,
        mesh=mesh,
        in_specs=placed,
        out_specs=(P("bank", None, None, "freq", None), P("bank", "freq", None)),
        check_vma=False,
    )
```

profile of v0, /device:TPU:0, one launch (start us, length us, event | category | flops | bytes accessed | tf_op | source)
XLA Modules:
  0.0 1100.0 jit_solution(13067060942839412740)
XLA Ops:
  11.7 40.7 %psum.7 = f32[2,32]{1,0:T(2,128)S(1)} all-reduce(f32[2,32]{1,0:T(2,128)S(1)} %reduce_sum.65), channel_id=1, replica_groups=mesh['bank'=8,'freq'=16] {'freq'}, use_global_device_ids=true, to_apply=%region_2.0 | all-reduce | flops 64 | bytes 512 | tf_op jit(solution)/shard_map/psum | solution.py:37
  80.8 9.0 fusion.40
  89.8 73.4 %fusion.6 = f32[2,3,32,2048]{3,2,1,0:T(8,128)S(1)} fusion(f32[2,3,32,2048]{3,2,1,0:T(8,128)S(1)} %copy-done.4), kind=kOutput, calls=%fused_computation.12 | convolution fusion | flops 9722396672 | bytes 3145728 | tf_op jit(solution)/shard_map/tdck,kn->tdcn/dot_general | solution.py:46
  163.2 73.6 %fusion.8 = f32[2,3,32,2048]{3,2,1,0:T(8,128)S(1)} fusion(f32[2,3,32,2048]{3,2,1,0:T(8,128)S(1)} %copy-done.5), kind=kOutput, calls=%fused_computation.14 | convolution fusion | flops 9722396672 | bytes 3145728 | tf_op jit(solution)/shard_map/tdck,kn->tdcn/dot_general | solution.py:43
  236.9 74.3 %fusion.49 = f32[2,3,32,2048]{3,2,1,0:T(8,128)S(1)} fusion(f32[2,3,32,2048]{3,2,1,0:T(8,128)S(1)} %fusion.8, f32[2,3,32,2048]{3,2,1,0:T(8,128)S(1)} %copy-done.3), kind=kOutput, calls=%fused_computation.51 | convolution fusion | flops 9722789888 | bytes 4718592 | tf_op jit(solution)/shard_map/tdck,kn->tdcn/dot_general | solution.py:43
  311.2 74.3 %add_multiply_fusion = (f32[2,3,32,2048]{3,2,1,0:T(8,128)S(1)}, f32[2,3,32,2048]{3,2,1,0:T(8,128)S(1)}) fusion(f32[2,3,32,2048]{3,2,1,0:T(8,128)S(1)} %fusion.49, f32[2]{0:T(128)S(1)} %get-tuple-element.30, f32[32,2048]{1,0:T(8,128)S(1)} %copy-done.7, f32[32,2048]{1,0:T(8,128)S(1)} %get-tuple-element.31, f32[2,3,32,2048]{3,2,1,0:T(8,128)S(1)} %fusion.6, ...), kind=kOutput, calls=%fused_computation.57 | convolution fusion | flops 9725935616 | bytes 8388616 | tf_op jit(solution)/shard_map/tdck,kn->tdcn/dot_general | solution.py:46
  419.5 77.1 %fusion.26 = f32[32,2048,32]{1,2,0:T(8,128)S(1)} fusion(s32[32,64]{1,0:T(8,128)S(1)} %multiply_add_fusion.4, f32[1,32,32,64,1]{3,0,4,2,1:T(1,128)S(1)} %copy-done.9), kind=kOutput, calls=%fused_computation.34 | convolution fusion | flops 1669332992 | bytes 8658944 | tf_op jit(solution)/shard_map/jcbk,bkn->jbcn/dot_general | solution.py:79
  496.6 78.7 %add_bitcast_fusion = f32[32,32,2048]{2,1,0:T(8,128)} fusion(f32[32,2048,32]{1,2,0:T(8,128)S(1)} %fusion.26, s32[32,64]{1,0:T(8,128)S(1)} %multiply_add_fusion.4, f32[1,32,32,64,1]{3,0,4,2,1:T(1,128)S(1)} %copy-done.10), kind=kOutput, calls=%fused_computation.30 | convolution fusion | flops 1671430144 | bytes 17047552 | tf_op jit(solution)/shard_map/jcbk,bkn->jbcn/dot_general | solution.py:79
  575.3 77.9 %fusion.28 = f32[32,2048,32]{1,2,0:T(8,128)} fusion(s32[32,64]{1,0:T(8,128)S(1)} %multiply_add_fusion.4, f32[1,32,32,64,1]{3,0,4,2,1:T(1,128)S(1)} %copy-done.10), kind=kOutput, calls=%fused_computation.35 | convolution fusion | flops 1669332992 | bytes 8658944 | tf_op jit(solution)/shard_map/jcbk,bkn->jbcn/dot_general | solution.py:76
  660.9 79.4 %subtract_bitcast_fusion = f32[32,32,2048]{2,1,0:T(8,128)S(1)} fusion(f32[32,2048,32]{1,2,0:T(8,128)} %fusion.28, s32[32,64]{1,0:T(8,128)S(1)} %multiply_add_fusion.4, f32[1,32,32,64,1]{3,0,4,2,1:T(1,128)} %fusion.40), kind=kOutput, calls=%fused_computation.31 | convolution fusion | flops 1671430144 | bytes 17047552 | tf_op jit(solution)/shard_map/jcbk,bkn->jbcn/dot_general | solution.py:76
  740.4 12.1 %fusion.20 = f32[16,32,2048]{2,0,1:T(8,128)S(1)} fusion(f32[32,32,2048]{2,1,0:T(8,128)} %add_bitcast_fusion, f32[32,16]{1,0:T(8,128)S(1)} %copy-done.11), kind=kOutput, calls=%fused_computation.26 | convolution fusion | flops 402653184 | bytes 12584960 | tf_op jit(solution)/shard_map/jbcn,jbl->jlcn/dot_general | solution.py:86
  752.5 11.6 %multiply_bitcast_fusion = (f32[1,16,32,2048]{3,1,2,0:T(8,128)}, f32[1,16,32,2048]{3,1,2,0:T(8,128)}) fusion(f32[16,32,2048]{2,0,1:T(8,128)S(1)} %fusion.20, f32[]{:T(128)} %get-tuple-element.29, f32[32,2048]{1,0:T(8,128)S(1)} %copy-done.8, f32[32,2048]{1,0:T(8,128)S(1)} %get-tuple-element.31, f32[32,32,2048]{2,1,0:T(8,128)S(1)} %subtract_bitcast_fusion, ...), kind=kOutput, calls=%fused_computation.45 | convolution fusion | flops 411041792 | bytes 21497860 | tf_op jit(solution)/shard_map/jbcn,jbl->jlcn/dot_general | solution.py:85
  764.2 12.9 %copy.127 = f32[1,16,32,2048]{2,1,0,3:T(8,128)} copy(f32[1,16,32,2048]{3,1,2,0:T(8,128)} %get-tuple-element.15) | data formatting | bytes 8388608 | tf_op jit(solution)/shard_map/mul | solution.py:88
  777.1 16.0 %reshape.257 = f32[16,1,65536]{2,1,0:T(1,128)} reshape(f32[2048,1,16,32]{3,2,1,0:T(8,128)} %bitcast.191) | data formatting | bytes 8388608
  800.4 12.9 %copy.131 = f32[1,16,32,2048]{2,1,0,3:T(8,128)} copy(f32[1,16,32,2048]{3,1,2,0:T(8,128)} %get-tuple-element.14) | data formatting | bytes 8388608 | tf_op jit(solution)/shard_map/mul | solution.py:89
  813.4 16.0 %reshape.259 = f32[16,1,65536]{2,1,0:T(1,128)} reshape(f32[2048,1,16,32]{3,2,1,0:T(8,128)} %bitcast.192) | data formatting | bytes 8388608
  829.4 19.3 %all-to-all-done.2 = f32[16,1,65536]{2,1,0:T(1,128)} async-done(((f32[16,1,65536]{2,1,0:T(1,128)}), f32[16,1,65536]{2,1,0:T(1,128)}, u32[]{:S(2)}, u32[]{:S(2)}) %all-to-all-start.2) | async-done | bytes 4194336 | tf_op jit(solution)/shard_map/all_to_all | solution.py:113
  868.5 9.0 copy.167
  897.0 9.2 fusion.67
  906.2 9.2 fusion.65
  915.4 9.6 subtract_bitcast_fusion.1
  925.0 9.4 add_bitcast_fusion.1
  936.6 13.7 %reduce.14 = f32[16,65536]{1,0:T(8,128)} reduce(f32[16,1,65536]{2,1,0:T(1,128)} %all-to-all-done.2, f32[]{:T(128)} %broadcast.258), dimensions={1}, to_apply=%all_to_all.56.reduce_sub_computation | reduce | bytes 8388612 | tf_op jit(solution)/shard_map/all_to_all | solution.py:113
  950.3 15.5 %reshape.258 = f32[2048,1,16,32]{3,2,1,0:T(8,128)} reshape(f32[16,65536]{1,0:T(8,128)} %reduce.14) | data formatting | bytes 8388608
  965.8 15.0 %copy.128 = f32[1,16,32,2048]{3,0,2,1:T(1,128)} copy(f32[1,16,32,2048]{2,1,0,3:T(8,128)} %bitcast.193) | data formatting | bytes 8388608 | tf_op jit(solution)/shard_map/all_to_all | solution.py:113
  984.3 18.4 %fusion.58 = f32[16,128,512]{2,1,0:T(8,128)} fusion(f32[16,512,128]{2,1,0:T(8,128)S(1)} %bitcast.197), kind=kOutput, calls=%fused_computation.68 | convolution fusion | flops 6446120960 | bytes 8388608 | tf_op jit(solution)/shard_map/...cn,cm->...nm/dot_general | solution.py:99
  1002.7 18.6 %fusion.62 = f32[16,128,512]{2,1,0:T(8,128)} fusion(f32[16,512,128]{2,1,0:T(8,128)S(1)} %bitcast.198), kind=kOutput, calls=%fused_computation.72 | convolution fusion | flops 6446120960 | bytes 8388608 | tf_op jit(solution)/shard_map/...cn,cm->...nm/dot_general | solution.py:96
  1021.3 13.7 %reduce.15 = f32[16,65536]{1,0:T(8,128)} reduce(f32[16,1,65536]{2,1,0:T(1,128)} %all-to-all-done.3, f32[]{:T(128)} %broadcast.258), dimensions={1}, to_apply=%all_to_all.59.reduce_sub_computation | reduce | bytes 8388612 | tf_op jit(solution)/shard_map/all_to_all | solution.py:114
  1034.9 15.1 %reshape.260 = f32[2048,1,16,32]{3,2,1,0:T(8,128)} reshape(f32[16,65536]{1,0:T(8,128)} %reduce.15) | data formatting | bytes 8388608
  1050.0 15.4 %copy.132 = f32[1,16,32,2048]{3,0,2,1:T(1,128)} copy(f32[1,16,32,2048]{2,1,0,3:T(8,128)} %bitcast.194) | data formatting | bytes 8388608 | tf_op jit(solution)/shard_map/all_to_all | solution.py:114
  1069.1 11.0 %fusion.190 = (f32[128,512]{1,0:T(8,128)S(1)}, f32[16,128,512]{2,1,0:T(8,128)S(1)}) fusion(f32[16,128,512]{2,1,0:T(8,128)S(1)} %copy-done.1, f32[16,512,128]{2,1,0:T(8,128)S(1)} %bitcast.195), kind=kOutput, calls=%fused_computation.213 | convolution fusion | flops 6448152576 | bytes 12845056 | tf_op jit(solution)/shard_map/...cn,cm->...nm/dot_general | solution.py:96
  1080.2 10.8 fusion.189
  (88 shorter events, 131.3 us)
Async XLA Ops:
  7.2 51.6 %all-gather.2.cloned.1.call-start = ((), (), s32[]{:S(2)}) async-start(), calls=%async_computation.4 | async-start | bytes 1769472 | tf_op jit(solution)/shard_map/all_gather | solution.py:22
  52.4 6.3 copy-start.14
  52.5 6.2 copy-start.16
  55.5 7.1 copy-start.12
  72.0 17.8 %copy-start.4 = (f32[2,3,32,2048]{3,2,1,0:T(8,128)S(1)}, f32[2,3,32,2048]{3,2,1,0:T(8,128)}, u32[]{:S(2)}) copy-start(f32[2,3,32,2048]{3,2,1,0:T(8,128)} %multiply_subtract_fusion.10) | copy-start | bytes 4718596
  89.8 73.4 %copy-start.5 = (f32[2,3,32,2048]{3,2,1,0:T(8,128)S(1)}, f32[2,3,32,2048]{3,2,1,0:T(8,128)}, u32[]{:S(2)}) copy-start(f32[2,3,32,2048]{3,2,1,0:T(8,128)} %multiply_add_fusion.8) | copy-start | bytes 4718596
  163.2 73.6 %copy-start.3 = (f32[2,3,32,2048]{3,2,1,0:T(8,128)S(1)}, f32[2,3,32,2048]{3,2,1,0:T(8,128)}, u32[]{:S(2)}) copy-start(f32[2,3,32,2048]{3,2,1,0:T(8,128)} %multiply_subtract_fusion.11) | copy-start | bytes 4718596
  236.9 74.4 %copy-start.2 = (f32[2,3,32,2048]{3,2,1,0:T(8,128)S(1)}, f32[2,3,32,2048]{3,2,1,0:T(8,128)}, u32[]{:S(2)}) copy-start(f32[2,3,32,2048]{3,2,1,0:T(8,128)} %multiply_add_fusion.2.clone.5) | copy-start | bytes 4718596
  236.9 74.4 %copy-start.7 = (f32[32,2048]{1,0:T(8,128)S(1)}, f32[32,2048]{1,0:T(8,128)}, u32[]{:S(2)}) copy-start(f32[32,2048]{1,0:T(8,128)} %get-tuple-element.32) | copy-start | bytes 786436
  400.6 252.7 %all-to-all-start.1 = ((f32[16,1,24576]{2,1,0:T(1,128)}), f32[16,1,24576]{2,1,0:T(1,128)S(1)}, u32[]{:S(2)}, u32[]{:S(2)}) async-start(f32[16,1,24576]{2,1,0:T(1,128)} %reshape.255), calls=%async_computation.1 | async-start | bytes 3145728 | tf_op jit(solution)/shard_map/all_to_all | solution.py:107
  411.1 8.4 copy-start.9
  419.5 77.1 %copy-start.10 = (f32[1,32,32,64,1]{3,0,4,2,1:T(1,128)S(1)}, f32[1,32,32,64,1]{3,0,4,2,1:T(1,128)}, u32[]{:S(2)}) copy-start(f32[1,32,32,64,1]{3,0,4,2,1:T(1,128)} %fusion.42) | copy-start | bytes 786436
  653.3 139.8 %all-to-all-start = ((f32[16,1,24576]{2,1,0:T(1,128)}), f32[16,1,24576]{2,1,0:T(1,128)S(1)}, u32[]{:S(2)}, u32[]{:S(2)}) async-start(f32[16,1,24576]{2,1,0:T(1,128)} %reshape.253), calls=%async_computation | async-start | bytes 3145728 | tf_op jit(solution)/shard_map/all_to_all | solution.py:106
  660.9 79.4 %copy-start.11 = (f32[32,16]{1,0:T(8,128)S(1)}, f32[32,16]{1,0:T(8,128)}, u32[]{:S(2)}) copy-start(f32[32,16]{1,0:T(8,128)} %select_reduce_fusion) | copy-start | bytes 6148
  740.4 12.1 %copy-start.8 = (f32[32,2048]{1,0:T(8,128)S(1)}, f32[32,2048]{1,0:T(8,128)}, u32[]{:S(2)}) copy-start(f32[32,2048]{1,0:T(8,128)} %get-tuple-element.32) | copy-start | bytes 786436
  793.1 55.6 %all-to-all-start.2 = ((f32[16,1,65536]{2,1,0:T(1,128)}), f32[16,1,65536]{2,1,0:T(1,128)}, u32[]{:S(2)}, u32[]{:S(2)}) async-start(f32[16,1,65536]{2,1,0:T(1,128)} %reshape.257), calls=%async_computation.2 | async-start | bytes 8388608 | tf_op jit(solution)/shard_map/all_to_all | solution.py:113
  829.4 24.0 %copy-start.13 = (s32[2,32]{1,0:T(2,128)S(1)}, s32[2,32]{1,0:T(2,128)}, u32[]{:S(2)}) copy-start(s32[2,32]{1,0:T(2,128)} %copy-done.12) | copy-start | bytes 772
  829.4 24.0 %copy-start.15 = (f32[2,32]{1,0:T(2,128)S(1)}, f32[2,32]{1,0:T(2,128)}, u32[]{:S(2)}) copy-start(f32[2,32]{1,0:T(2,128)} %copy-done.14) | copy-start | bytes 772
  829.4 24.3 %copy-start.17 = (f32[2]{0:T(128)S(1)}, f32[2]{0:T(128)}, u32[]{:S(2)}) copy-start(f32[2]{0:T(128)} %copy-done.16) | copy-start | bytes 28
  848.6 172.6 %all-to-all-start.3 = ((f32[16,1,65536]{2,1,0:T(1,128)}), f32[16,1,65536]{2,1,0:T(1,128)}, u32[]{:S(2)}, u32[]{:S(2)}) async-start(f32[16,1,65536]{2,1,0:T(1,128)} %reshape.259), calls=%async_computation.3 | async-start | bytes 8388608 | tf_op jit(solution)/shard_map/all_to_all | solution.py:114
  897.0 18.4 %copy-start.6 = (f32[2,3,32,16,128]{4,2,3,1,0:T(8,128)S(1)}, f32[2,3,32,16,128]{4,2,3,1,0:T(8,128)}, u32[]{:S(2)}) copy-start(f32[2,3,32,16,128]{4,2,3,1,0:T(8,128)} %copy.167) | copy-start | bytes 4718596
  1065.4 3.7 copy-start.1
  1069.1 11.0 %copy-start = (f32[16,128,512]{2,1,0:T(8,128)S(1)}, f32[16,128,512]{2,1,0:T(8,128)}, u32[]{:S(2)}) copy-start(f32[16,128,512]{2,1,0:T(8,128)} %fusion.58) | copy-start | bytes 12582916
Sparse Core Ops, SparseCore 0:
  9.7 27.1 all-gather.1
where the time goes:
time: 1110 us; the launch traced here: 1100 us
  matrix products  747 us (67%)
  local copies, waits for them, and re-layouts  199 us (18%)
  other arithmetic  53.4 us (5%)
  blocking collectives  40.7 us (4%)
  starting transfers between devices  23.7 us (2%)
  waiting for transfers between devices  20 us (2%)
  between operations  15.9 us (1%)
    unnamed x46, local copies, waits for them, and re-layouts  97.7 us
    dot_general x1, matrix products, per_device(): jnp.einsum(form_block, entry_im, block_sin, precision=highest)  79.4 us
    dot_general x1, matrix products, per_device(): jnp.einsum(form_block, entry_re, block_sin, precision=highest)  78.7 us
    dot_general x1, matrix products, per_device(): jnp.einsum(form_block, entry_re, block_cos, precision=highest)  77.9 us
    dot_general x1, matrix products, per_device(): jnp.einsum(form_block, entry_im, block_cos, precision=highest)  77.1 us
    dot_general x1, matrix products, per_device(): jnp.einsum(form, prod_im, first_sin, precision=highest)  74.3 us
    dot_general x1, matrix products, per_device(): jnp.einsum(form, prod_re, first_sin, precision=highest)  74.3 us
    dot_general x1, matrix products, per_device(): jnp.einsum(form, prod_re, first_cos, precision=highest)  73.6 us
  transfers between devices with their start and end apart: 5, of which 1 were waited for; matrix products, arithmetic and copies ran while one was open for 53% of the time, Pallas kernels for 0%

commit v1 on v0

v1 whole, which is shorter than its diff:
```python
import math

import jax
import jax.numpy as jnp
import numpy as np
from jax import lax
from jax.experimental import pallas as pl
from jax.experimental.pallas import tpu as pltpu
from jax.sharding import PartitionSpec as P

N1 = 2048
N2 = 512
DET = 3
NBLK = 32
BINS = 16
BF = jnp.bfloat16
F32 = jnp.float32
ANY = pl.BlockSpec(memory_space=pl.ANY)
SMEM = pl.BlockSpec(memory_space=pltpu.SMEM)
MESH = pl.DeviceIdType.MESH


def split(value):
    high = value.astype(BF)
    return high, (value - high.astype(F32)).astype(BF)


def radix4(x):
    (ar, ai), (br, bi), (cr, ci), (dr, di) = x
    pr, pi, mr, mi = ar + cr, ai + ci, ar - cr, ai - ci
    sr, si, tr, ti = br + dr, bi + di, br - dr, bi - di
    return [(pr + sr, pi + si), (mr - ti, mi + tr), (pr - sr, pi - si), (mr + ti, mi - tr)]


def times(x, c, s):
    return x[0] * c - x[1] * s, x[0] * s + x[1] * c


def radix16(x):
    mid = [radix4([x[low + 4 * high] for high in range(4)]) for low in range(4)]
    out = [None] * 16
    for first in range(4):
        row = []
        for low in range(4):
            angle = 2.0 * math.pi * low * first / 16
            value = mid[low][first]
            row.append(value if low * first == 0 else times(value, math.cos(angle), math.sin(angle)))
        for second, value in enumerate(radix4(row)):
            out[first + 4 * second] = value
    return out


def gather_bank_kernel(own, out, send, recv, local):
    me = lax.axis_index("bank")
    z, core = me // 2, lax.rem(me, 2)
    up = lax.rem(z + 1, 4) * 2 + core
    down = lax.rem(z + 3, 4) * 2 + core
    far = lax.rem(z + 2, 4) * 2 + core
    twin = z * 2 + 1 - core
    barrier = pltpu.get_barrier_semaphore()
    for peer in (up, down, twin):
        pl.semaphore_signal(barrier, inc=1, device_id={"bank": peer}, device_id_type=MESH)
    pl.semaphore_wait(barrier, 3)
    half = own.shape[0] // 2
    sent = []

    def piece(owner, k):
        return out.at[owner, pl.ds(k * half, half)]

    def go(owner, k, peer, first=False):
        copy = pltpu.make_async_remote_copy(
            src_ref=own.at[pl.ds(k * half, half)] if first else piece(owner, k),
            dst_ref=piece(owner, k),
            send_sem=send.at[len(sent)],
            recv_sem=recv.at[owner, k],
            device_id={"bank": peer},
            device_id_type=MESH,
        )
        copy.start()
        sent.append(copy)

    def arrived(owner, k):
        pltpu.make_async_copy(piece(owner, k), piece(owner, k), recv.at[owner, k]).wait()

    keep = pltpu.make_async_copy(own, out.at[me], local)
    keep.start()
    go(me, 0, up, True)
    go(me, 1, down, True)
    go(me, 1, up, True)
    go(me, 0, down, True)
    go(me, 0, twin, True)
    go(me, 1, twin, True)
    arrived(down, 0)
    go(down, 0, up)
    arrived(up, 1)
    go(up, 1, down)
    go(down, 0, twin)
    go(up, 1, twin)
    arrived(down, 1)
    go(down, 1, twin)
    arrived(up, 0)
    go(up, 0, twin)
    arrived(far, 0)
    go(far, 0, twin)
    arrived(far, 1)
    go(far, 1, twin)
    for step in (0, 1, 3, 2):
        for k in (0, 1):
            arrived(lax.rem(z + step, 4) * 2 + 1 - core, k)
    keep.wait()
    for copy in sent:
        copy.wait_send()


def gather_bank(own):
    return pl.pallas_call(
        gather_bank_kernel,
        out_shape=jax.ShapeDtypeStruct((8,) + own.shape, own.dtype),
        in_specs=[ANY],
        out_specs=ANY,
        scratch_shapes=[
            pltpu.SemaphoreType.DMA((14,)),
            pltpu.SemaphoreType.DMA((8, 2)),
            pltpu.SemaphoreType.DMA,
        ],
        compiler_params=pltpu.CompilerParams(collective_id=2, has_side_effects=True),
        name="gather_bank",
    )(own)


def gather_freq_kernel(own, small, out, small_out, send, recv, local):
    me = lax.axis_index("freq")
    my, mx = me // 4, lax.rem(me, 4)

    def place(axis, along, across):
        dx, dy = (along, across) if axis == "x" else (across, along)
        return lax.rem(my + dy + 4, 4) * 4 + lax.rem(mx + dx + 4, 4)

    barrier = pltpu.get_barrier_semaphore()
    for axis in "xy":
        for off in (1, -1):
            pl.semaphore_signal(
                barrier, inc=1, device_id={"freq": place(axis, off, 0)}, device_id_type=MESH
            )
    pl.semaphore_wait(barrier, 4)
    rows = own.shape[0] // 4
    plans = [("x", "y", 1), ("y", "x", 1), ("x", "y", -1), ("y", "x", -1), ("x", "y", 1)]
    sent = []
    counts = [0] * 5

    def piece(p, owner):
        return small_out.at[owner] if p == 4 else out.at[owner, pl.ds(p * rows, rows)]

    def go(p, owner, axis, off, first=False):
        mine = small if p == 4 else own.at[pl.ds(p * rows, rows)]
        copy = pltpu.make_async_remote_copy(
            src_ref=mine if first else piece(p, owner),
            dst_ref=piece(p, owner),
            send_sem=send.at[p, counts[p]],
            recv_sem=recv.at[p, owner],
            device_id={"freq": place(axis, off, 0)},
            device_id_type=MESH,
        )
        counts[p] += 1
        copy.start()
        sent.append(copy)

    def arrived(p, owner):
        pltpu.make_async_copy(piece(p, owner), piece(p, owner), recv.at[p, owner]).wait()

    keep = [
        pltpu.make_async_copy(own, out.at[me], local.at[0]),
        pltpu.make_async_copy(small, small_out.at[me], local.at[1]),
    ]
    for copy in keep:
        copy.start()
    order = list(enumerate(plans))
    for p, (first, second, s) in order:
        go(p, me, first, s, True)
        go(p, me, first, -s, True)
    for p, (first, second, s) in order:
        go(p, me, second, s, True)
        go(p, me, second, -s, True)
    for p, (first, second, s) in order:
        owner = place(first, -s, 0)
        arrived(p, owner)
        go(p, owner, first, s)
        go(p, owner, second, s)
        go(p, owner, second, -s)
    for p, (first, second, s) in order:
        owner = place(first, s, 0)
        arrived(p, owner)
        go(p, owner, second, s)
        go(p, owner, second, -s)
    for p, (first, second, s) in order:
        owner = place(first, 0, -s)
        arrived(p, owner)
        go(p, owner, second, s)
    for p, (first, second, s) in order:
        owner = place(first, 2, 0)
        arrived(p, owner)
        go(p, owner, second, s)
        go(p, owner, second, -s)
    for along in (-1, 1, 2):
        for p, (first, second, s) in order:
            owner = place(first, along * s, -s)
            arrived(p, owner)
            go(p, owner, second, s)
    for along in (0, -1, 1, 2):
        for across in (1, 2):
            for p, (first, second, s) in order:
                arrived(p, place(first, along * s, across * s))
    for copy in keep:
        copy.wait()
    for copy in sent:
        copy.wait_send()


def gather_freq(own, small):
    return pl.pallas_call(
        gather_freq_kernel,
        out_shape=(
            jax.ShapeDtypeStruct((16,) + own.shape, own.dtype),
            jax.ShapeDtypeStruct((16,) + small.shape, small.dtype),
        ),
        in_specs=[ANY, ANY],
        out_specs=(ANY, ANY),
        scratch_shapes=[
            pltpu.SemaphoreType.DMA((5, 15)),
            pltpu.SemaphoreType.DMA((5, 16)),
            pltpu.SemaphoreType.DMA((2,)),
        ],
        compiler_params=pltpu.CompilerParams(collective_id=1, has_side_effects=True),
        cost_estimate=pl.CostEstimate(flops=0, bytes_accessed=200_000_000, transcendentals=0),
        name="gather_freq",
    )(own, small)


def front_kernel(
    tmpl_pick, det_pick, strain, tmpl, spin_c, spin_s, dft, twist_c, twist_s,
    entry, power, outgoing, spread, turned,
):
    t_pick = tmpl_pick[0]
    d_pick = det_pick[0]
    lane = lax.broadcasted_iota(jnp.int32, (8, 128), 1)
    left = lane < 64

    def product(t, d, rows, a):
        half = pl.ds((a % 2) * 128, 128)
        lanes = pl.ds(a * 128, 128)
        hr, hi = tmpl[t, 0, rows, lanes], tmpl[t, 1, rows, lanes]
        sr, si = strain[a // 2, 2 * d, rows, half], strain[a // 2, 2 * d + 1, rows, half]
        return hr * sr + hi * si, hr * si - hi * sr

    @pl.loop(0, 4)
    def _(chunk):
        rows = pl.ds(pl.multiple_of(chunk * 8, 8), 8)
        for a in range(16):
            re, im = product(t_pick, d_pick, rows, a)
            re_far, im_far = pltpu.roll(re, 64, 1), pltpu.roll(im, 64, 1)
            entry[rows, 256 * a : 256 * a + 128] = jnp.where(left, re, im_far)
            entry[rows, 256 * a + 128 : 256 * a + 256] = jnp.where(left, re_far, im)

    col = lax.broadcasted_iota(jnp.int32, (128, 128), 1)
    depth = lax.broadcasted_iota(jnp.int32, (128, 128), 0)
    total = jnp.zeros((8, 128), F32)
    for t in range(2):
        for g in range(2):
            sums = []
            for a in range(8 * g, 8 * g + 8):
                lanes = pl.ds(a * 128, 128)
                hr, hi = tmpl[t, 0, :, lanes], tmpl[t, 1, :, lanes]
                sums.append(jnp.sum(hr * hr + hi * hi, axis=0, keepdims=True))
            select = (col == 4 * t + 2 * g + depth // 64).astype(F32)
            total += jnp.dot(
                jnp.concatenate(sums, axis=0),
                select,
                precision=lax.Precision.HIGHEST,
                preferred_element_type=F32,
            )
    power[...] = total

    @pl.loop(0, 24)
    def _(step):
        series = step // 4
        t, d = series // 3, lax.rem(series, 3)
        rows = pl.ds(pl.multiple_of(lax.rem(step, 4) * 8, 8), 8)
        where = pl.ds(pl.multiple_of(step * 8, 8), 8)
        result = radix16([product(t, d, rows, a) for a in range(16)])
        for q in range(16):
            re, im = result[q]
            if q:
                re, im = times((re, im), spin_c[q], spin_s[q])
            spread[q, where, 0:128] = re
            spread[q, where, 128:256] = im

    spread[:, 192:256, :] = jnp.zeros((16, 64, 256), F32)

    @pl.loop(0, 16)
    def _(q):
        high, low = split(spread[q])
        stack = jnp.concatenate([high, low, high], axis=1)
        out = lax.dot_general(
            dft[...], stack, (((1,), (1,)), ((), ())), preferred_element_type=F32
        )
        for part in range(2):
            for h in range(2):
                turned[part, h, pl.ds(q, 128, stride=16), :] = out[
                    part * 128 : part * 128 + 128, h * 128 : h * 128 + 128
                ]

    @pl.loop(0, 16)
    def _(f):
        here = pl.ds(pl.multiple_of(f * 128, 128), 128)
        c, s = twist_c[:, here], twist_s[:, here]
        for h in range(2):
            re = turned[0, h, here, :].T
            im = turned[1, h, here, :].T
            for k in range(4 - 2 * h):
                rows = slice(32 * k, 32 * k + 32)
                out_re, out_im = times((re[rows], im[rows]), c, s)
                base = 128 * h + 32 * k
                outgoing[f, base : base + 32, :] = out_re
                outgoing[f, 192 + base : 192 + base + 32, :] = out_im


def front(tmpl_pick, det_pick, strain, tmpl, spin, dft, twist):
    return pl.pallas_call(
        front_kernel,
        out_shape=(
            jax.ShapeDtypeStruct((32, 2 * N1), F32),
            jax.ShapeDtypeStruct((8, 128), F32),
            jax.ShapeDtypeStruct((16, 384, 128), F32),
        ),
        in_specs=[SMEM, SMEM] + [pl.BlockSpec(memory_space=pltpu.VMEM)] * 7,
        out_specs=[pl.BlockSpec(memory_space=pltpu.VMEM)] * 3,
        scratch_shapes=[
            pltpu.VMEM((16, 256, 256), F32),
            pltpu.VMEM((2, 2, N1, 128), F32),
        ],
        compiler_params=pltpu.CompilerParams(vmem_limit_bytes=48 << 20),
        name="front",
    )(tmpl_pick, det_pick, strain, tmpl, *spin, dft, *twist)


def second_section(load, turn_c, turn_s, dft_hh, dft_l, stage_hl):
    @pl.loop(0, 8)
    def _(chunk):
        halves = []
        for sub in range(2):
            row = pl.multiple_of(chunk * 16 + sub * 8, 8)
            result = radix4([load(a, row) for a in range(4)])
            here = pl.ds(row, 8)
            for q in range(1, 4):
                result[q] = times(result[q], turn_c[q - 1, here, :], turn_s[q - 1, here, :])
            halves.append(result)
        row16 = pl.multiple_of(chunk * 16, 16)
        for q in range(4):
            for part in range(2):
                value = jnp.concatenate([halves[0][q][part], halves[1][q][part]], axis=0)
                high, low = split(value)
                lanes = slice(128 * q, 128 * q + 128)
                stage_hl[pl.ds(row16 + 128 * part, 16), lanes] = high
                stage_hl[pl.ds(row16 + 256 + 128 * part, 16), lanes] = low

    return jnp.dot(dft_hh[...], stage_hl[...], preferred_element_type=F32) + jnp.dot(
        dft_l[...], stage_hl[0:256, :], preferred_element_type=F32
    )


def sum_power(power):
    total = power[0]
    for f in range(1, 16):
        total = total + power[f]
    return total


def power_maps():
    col = lax.broadcasted_iota(jnp.int32, (8, 128), 1)
    row = lax.broadcasted_iota(jnp.int32, (8, 128), 0)
    block = 2 * (row + 8 * (lax.rem(col, 4) // 2)) + lax.rem(col, 2)
    return block, col // 4


def chi_kernel(
    tmpl_pick, bin_of, edges, gathered, power, base_c, base_s, step_c, step_s, twist_c, twist_s,
    turn_c, turn_s, dft_hh, dft_l, out, sections, series, stage_hl, total, weight_s, order,
):
    t = tmpl_pick[0]
    all_power = sum_power(power)
    block, owner = power_maps()
    mine = jnp.where(owner == t, all_power, 0.0)
    sigma_sq = jnp.sum(mine, keepdims=True)
    for level in range(BINS):
        low = 0 if level == 0 else edges[t, level - 1]
        high = NBLK if level == BINS - 1 else edges[t, level]
        inside = (block >= low) & (block < high)
        bin_power = jnp.sum(jnp.where(inside, mine, 0.0), keepdims=True)
        weight_s[level] = jnp.broadcast_to(bin_power / sigma_sq, (8, 128))

    @pl.loop(0, NBLK)
    def _(b):
        pc, ps = step_c[pl.ds(b, 1), :], step_s[pl.ds(b, 1), :]
        wr, wi = times((base_c[...], base_s[...]), pc, ps)
        matrix = jnp.concatenate(
            [jnp.concatenate([wr, wi], axis=1), jnp.concatenate([-wi, wr], axis=1)], axis=0
        )
        m_high, m_low = split(matrix)
        value = gathered[:, :, pl.ds(pl.multiple_of(b * 128, 128), 128)].reshape(N2, 128)
        high, low = split(value)
        section = jnp.dot(
            jnp.concatenate([high, low], axis=1),
            jnp.concatenate([m_high, m_high], axis=0),
            preferred_element_type=F32,
        ) + jnp.dot(high, m_low, preferred_element_type=F32)
        level = bin_of[t, b]
        fresh = (b == 0) | (bin_of[t, jnp.maximum(b - 1, 0)] != level)

        @pl.when(fresh)
        def _():
            sections[level] = section

        @pl.when(jnp.logical_not(fresh))
        def _():
            sections[level] += section

    @pl.loop(0, BINS)
    def _(level):
        def load(a, row):
            here = pl.ds(a * 128 + row, 8)
            value = (sections[level, here, 0:128], sections[level, here, 128:256])
            return times(value, twist_c[here, :], twist_s[here, :])

        result = second_section(load, turn_c, turn_s, dft_hh, dft_l, stage_hl)
        series[level] = result

        @pl.when(level == 0)
        def _():
            total[...] = result

        @pl.when(level > 0)
        def _():
            total[...] += result

    inv = 1.0 / sigma_sq

    @pl.loop(0, 16)
    def _(chunk):
        row = pl.multiple_of(chunk * 8, 8)
        for q in range(4):
            lanes = slice(128 * q, 128 * q + 128)
            whole_re = total[pl.ds(row, 8), lanes]
            whole_im = total[pl.ds(128 + row, 8), lanes]
            sums = jnp.zeros((8, 128), F32)
            for level in range(BINS):
                weight = weight_s[level]
                dev_re = series[level, pl.ds(row, 8), lanes] - weight * whole_re
                dev_im = series[level, pl.ds(128 + row, 8), lanes] - weight * whole_im
                sums += (dev_re * dev_re + dev_im * dev_im) * (1.0 / weight)
            order[pl.ds(q + 4 * row, 8, stride=4), :] = sums * inv

    out[0] = order[...].T


def chi(tmpl_pick, bin_of, edges, gathered, power, base, step, twist, turn, dft_hh, dft_l):
    vmem = pl.BlockSpec(memory_space=pltpu.VMEM)
    return pl.pallas_call(
        chi_kernel,
        out_shape=jax.ShapeDtypeStruct((1, 128, N2), F32),
        in_specs=[SMEM] * 3 + [vmem] * 12,
        out_specs=vmem,
        scratch_shapes=[
            pltpu.VMEM((BINS, N2, 256), F32),
            pltpu.VMEM((BINS, 256, N2), F32),
            pltpu.VMEM((512, N2), BF),
            pltpu.VMEM((256, N2), F32),
            pltpu.VMEM((BINS, 8, 128), F32),
            pltpu.VMEM((N2, 128), F32),
        ],
        compiler_params=pltpu.CompilerParams(vmem_limit_bytes=48 << 20),
        cost_estimate=pl.CostEstimate(flops=20_000_000_000, bytes_accessed=9_000_000, transcendentals=0),
        name="chi",
    )(tmpl_pick, bin_of, edges, gathered, power, *base, *step, *twist, *turn, dft_hh, dft_l)


def snr_kernel(in_re, in_im, power, turn_c, turn_s, dft_hh, dft_l, out, stage_hl, order):
    t = pl.program_id(0) // DET
    _, owner = power_maps()
    sigma_sq = jnp.sum(jnp.where(owner == t, sum_power(power), 0.0), keepdims=True)
    inv = 1.0 / jnp.sqrt(sigma_sq)

    def load(a, row):
        source = 4 * a + row // 32
        here = pl.ds(lax.rem(row, 32), 8)
        return in_re[source, here, :], in_im[source, here, :]

    result = second_section(load, turn_c, turn_s, dft_hh, dft_l, stage_hl) * inv
    for part in range(2):
        for q in range(4):
            order[pl.ds(q, 128, stride=4), :] = result[
                part * 128 : part * 128 + 128, q * 128 : q * 128 + 128
            ]
        out[0, 0, part] = order[...].T


def snr_of(arrived, power, turn, dft_hh, dft_l):
    whole = lambda *shape: pl.BlockSpec(shape, lambda i: (0,) * len(shape))
    return pl.pallas_call(
        snr_kernel,
        out_shape=jax.ShapeDtypeStruct((2, DET, 2, 128, N2), F32),
        grid=(6,),
        in_specs=[
            pl.BlockSpec((16, 32, 128), lambda i: (0, i, 0)),
            pl.BlockSpec((16, 32, 128), lambda i: (0, i + 6, 0)),
            whole(16, 8, 128),
            whole(3, 128, 128),
            whole(3, 128, 128),
            whole(256, 512),
            whole(256, 256),
        ],
        out_specs=pl.BlockSpec((1, 1, 2, 128, N2), lambda i: (i // DET, lax.rem(i, DET), 0, 0, 0)),
        scratch_shapes=[pltpu.VMEM((512, N2), BF), pltpu.VMEM((N2, 128), F32)],
        compiler_params=pltpu.CompilerParams(vmem_limit_bytes=32 << 20),
        name="snr",
    )(arrived, arrived, power, *turn, dft_hh, dft_l)


def turns(product, length):
    angle = (product % length).astype(F32) * (2.0 * math.pi / length)
    return jnp.cos(angle), jnp.sin(angle)


def fixed_turns(product, length):
    angle = 2.0 * np.pi * (product % length) / length
    return np.cos(angle), np.sin(angle)


def fixed_tables():
    index = np.arange(128)
    c, s = fixed_turns(index[:, None] * index[None, :], 128)
    full = np.concatenate(
        [np.concatenate([c, -s], axis=1), np.concatenate([s, c], axis=1)], axis=0
    ).astype(np.float32)
    high = full.astype(jnp.bfloat16)
    low = (full - high.astype(np.float32)).astype(jnp.bfloat16)
    spin = [
        np.ascontiguousarray(np.broadcast_to(v[:, None, :], (16, 8, 128))).astype(np.float32)
        for v in fixed_turns(np.arange(16)[:, None] * index[None, :], N1)
    ]
    turn = [
        np.ascontiguousarray(np.broadcast_to(v[:, :, None], (3, 128, 128))).astype(np.float32)
        for v in fixed_turns(np.arange(1, 4)[:, None] * index[None, :], N2)
    ]
    step = [
        v.astype(np.float32)
        for v in fixed_turns(np.arange(NBLK)[:, None] * index[None, :], NBLK)
    ]
    return high, low, spin, turn, step


def per_device(strain, templates, coinc_tmpl, coinc_det, bin_edges):
    high, low, spin, turn, step = fixed_tables()
    dft3 = np.concatenate([high, high, low], axis=1)
    dft_hh = np.concatenate([high, high], axis=1)
    place = lax.axis_index("freq")
    rows = place * 32 + jnp.arange(32, dtype=jnp.int32)
    times_all = jnp.arange(N1, dtype=jnp.int32)
    times_own = place * 128 + jnp.arange(128, dtype=jnp.int32)
    send_twist = turns(rows[:, None] * times_all[None, :], N1 * N2)
    own_twist = turns(jnp.arange(N2, dtype=jnp.int32)[:, None] * times_own[None, :], N1 * N2)
    base = turns(jnp.arange(64, dtype=jnp.int32)[:, None] * times_own[None, :], N1)
    bin_of = jnp.sum(
        jnp.arange(NBLK, dtype=jnp.int32)[None, :, None] >= bin_edges[:, None, :],
        axis=2,
        dtype=jnp.int32,
    )
    strain_all = gather_bank(strain.reshape(2 * DET, 32, 256))
    entry, power, outgoing = front(
        coinc_tmpl, coinc_det, strain_all, templates, spin, dft3, send_twist
    )
    arrived = lax.all_to_all(outgoing, "freq", 0, 0)
    gathered, power_all = gather_freq(entry, power)
    chi_sq = chi(
        coinc_tmpl, bin_of, bin_edges, gathered, power_all, base, step, own_twist, turn, dft_hh, low
    )
    snr = snr_of(arrived, power_all, turn, dft_hh, low)
    return (snr, chi_sq)


def solution(mesh):
    placed = (
        P(None, None, "freq", "bank"),
        P("bank", None, "freq", None),
        P("bank"),
        P("bank"),
        P("bank", None),
    )
    return jax.shard_map(
        per_device,
        mesh=mesh,
        in_specs=placed,
        out_specs=(P("bank", None, None, "freq", None), P("bank", "freq", None)),
        check_vma=False,
    )
```

time: 1110 us -> 180 us (0.16)
  matrix products: 747 us -> 0 us
  local copies, waits for them, and re-layouts: 199 us -> 13.7 us
  Pallas kernels: 0 us -> 154 us
  other arithmetic: 53.4 us -> 2.38 us
  blocking collectives: 40.7 us -> 0 us
  waiting for transfers between devices: 20 us -> 0.01 us
  starting transfers between devices: 23.7 us -> 7.19 us
  between operations: 15.9 us -> 2.05 us
    dot_general x22 -> x0, matrix products: 747 us -> none  [the longest x1 79.4 us: per_device(): jnp.einsum(form_block, entry_im, block_sin, precision=highest)]
    pallas_call x0 -> x5, Pallas kernels: none -> 154 us  [the longest x1 91 us: gather_freq(): pl.pallas_call(gather_freq_kernel, out_shape=(jax.ShapeDtypeStruct((16,)...]
    unnamed x46 -> x37, local copies, waits for them, and re-layouts: 97.7 us -> 13.7 us
    all_to_all x7 -> x0, local copies, waits for them, and re-layouts: 54.8 us -> none  [the longest x2 19.1 us: per_device(): lax.all_to_all(bins_im, 'freq', split_axis=3, concat_axis=2, tiled=True)]
    mul x9 -> x0, local copies, waits for them, and re-layouts: 46.8 us -> none  [the longest x1 12.9 us: per_device(): bins_im = (raw_re * twist_sin + raw_im * twist_cos) * slot_scale]
    psum x1 -> x0, blocking collectives: 40.7 us -> none  [per_device(): block_power = lax.psum(local_power, 'freq')]
    all_to_all x4 -> x0, other arithmetic: 37.8 us -> none  [the longest x1 13.7 us: per_device(): lax.all_to_all(bins_re, 'freq', split_axis=3, concat_axis=2, tiled=True)]
    all_to_all x4 -> x1, waiting for transfers between devices: 19.3 us -> 0.01 us  [per_device(): arrived = lax.all_to_all(outgoing, 'freq', 0, 0)]
  transfers between devices with their start and end apart: 5 -> 1, of which waited for: 1 -> 0; matrix products, arithmetic and copies ran while one was open for 53% -> 1% of each run, Pallas kernels for 0% -> 66%
where the time goes in v1:
time: 180 us; the launch traced here: 179 us
  Pallas kernels  154 us (86%)
  local copies, waits for them, and re-layouts  13.7 us (8%)
  starting transfers between devices  7.19 us (4%)
  other arithmetic  2.38 us (1%)
  between operations  2.05 us (1%)
    pallas_call x1, Pallas kernels, gather_freq(): pl.pallas_call(gather_freq_kernel, out_shape=(jax.ShapeDtypeStruct((16,)...  91 us
    pallas_call x1, Pallas kernels, chi(): pl.pallas_call(chi_kernel, out_shape=jax.ShapeDtypeStruct((1, 128, N2), F...  28 us
    pallas_call x1, Pallas kernels, gather_bank(): pl.pallas_call(gather_bank_kernel, out_shape=jax.ShapeDtypeStruct((8,) +...  14.8 us
    unnamed x37, local copies, waits for them, and re-layouts  13.7 us
    pallas_call x1, Pallas kernels, front(): pl.pallas_call(front_kernel, out_shape=(jax.ShapeDtypeStruct((32, 2 * N1)...  12.8 us
    all_to_all x1, starting transfers between devices, per_device(): arrived = lax.all_to_all(outgoing, 'freq', 0, 0)  7.19 us
    pallas_call x1, Pallas kernels, snr_of(): pl.pallas_call(snr_kernel, out_shape=jax.ShapeDtypeStruct((2, DET, 2, 128...  7 us
  transfers between devices with their start and end apart: 1, of which 0 were waited for; matrix products, arithmetic and copies ran while one was open for 1% of the time, Pallas kernels for 66%

profile of v1, /device:TPU:0, one launch (start us, length us, event | category | flops | bytes accessed | tf_op | source)
XLA Modules:
  0.0 178.9 jit_solution(3618939806778722255)
XLA Ops:
  0.6 1.1 fusion.14
  2.4 14.8 %gather_bank.1.strain = f32[8,6,32,256]{3,2,1,0:T(8,128)} custom-call(f32[6,32,256]{2,1,0:T(8,128)} %bitcast.1), custom_call_target="tpu_custom_call" | custom-call | tf_op jit(solution)/shard_map/gather_bank/pallas_call | solution.py:116
  17.9 0.0 copy-start
  17.9 1.4 copy-done
  19.3 1.2 copy-done.1
  20.5 1.0 copy-done.3
  21.5 0.8 copy-done.12
  22.3 0.8 copy-done.13
  23.2 12.8 %front.1 = (f32[32,4096]{1,0:T(8,128)S(1)}, f32[8,128]{1,0:T(8,128)S(1)}, f32[16,384,128]{2,1,0:T(8,128)}) custom-call(s32[1]{0:T(128)S(6)} %copy.17.tmpl_pick, s32[1]{0:T(128)S(6)} %copy.18.det_pick, f32[8,6,32,256]{3,2,1,0:T(8,128)S(1)} %copy-done, f32[2,2,32,2048]{3,2,1,0:T(8,128)S(1)} %copy-done.1, f32[16,8,128]{2,1,0:T(8,128)S(1)} %copy-done.12, ...), custom_call_target="tpu_custom_call" | custom-call | tf_op jit(solution)/shard_map/front/pallas_call | solution.py:328
  36.0 0.9 copy-done.2
  36.9 0.6 copy-done.14
  37.5 7.2 %all-to-all-start = ((f32[16,384,128]{2,1,0:T(8,128)}), f32[16,384,128]{2,1,0:T(8,128)S(1)}, u32[]{:S(2)}, u32[]{:S(2)}) async-start(f32[16,384,128]{2,1,0:T(8,128)} %get-tuple-element.7), calls=%async_computation | async-start | bytes 6291456 | tf_op jit(solution)/shard_map/all_to_all | solution.py:581
  44.7 0.0 copy-done.15
  44.7 0.1 copy.16
  44.8 91.0 %gather_freq.1 = (f32[16,32,4096]{2,1,0:T(8,128)}, f32[16,8,128]{2,1,0:T(8,128)}) custom-call(f32[32,4096]{1,0:T(8,128)} %copy-done.2, f32[8,128]{1,0:T(8,128)} %copy-done.14), custom_call_target="tpu_custom_call" | custom-call | bytes 200000000 | tf_op jit(solution)/shard_map/gather_freq/pallas_call | solution.py:220
  135.8 0.1 fusion.24.bin_of
  135.8 0.1 fusion.22
  136.0 1.0 fusion.12
  137.0 0.0 copy-done.4
  137.1 0.0 copy-done.9
  137.1 0.0 copy-start.5
  137.1 0.9 copy-done.5
  138.0 0.9 copy-done.7
  138.9 0.8 copy-done.10
  139.8 0.7 copy-done.16
  140.5 0.7 copy-done.17
  141.2 28.0 %chi.1 = f32[1,128,512]{2,1,0:T(8,128)} custom-call(s32[1]{0:T(128)S(6)} %copy.17.tmpl_pick, s32[2,32]{1,0:T(2,128)S(1)} %fusion.24.bin_of, s32[2,15]{1,0:T(2,128)S(1)} %copy-done.15, f32[16,32,4096]{2,1,0:T(8,128)} %get-tuple-element.11.gathered, f32[16,8,128]{2,1,0:T(8,128)S(1)} %copy-done.10, f32[64,128]{1,0:T(8,128)S(1)} %get-tuple-element.15.base_c, ...), custom_call_target="tpu_custom_call" | custom-call | flops 20000000000 | bytes 9000000 | tf_op jit(solution)/shard_map/chi/pallas_call | solution.py:467
  169.2 0.0 all-to-all-done.in_re.in_im
  169.2 0.9 copy-done.6
  170.1 0.9 copy-done.8
  171.0 0.8 copy-done.11
  171.9 7.0 %snr.1 = f32[2,3,2,128,512]{4,3,2,1,0:T(8,128)} custom-call(f32[16,384,128]{2,1,0:T(8,128)S(1)} %all-to-all-done.in_re.in_im, f32[16,384,128]{2,1,0:T(8,128)S(1)} %all-to-all-done.in_re.in_im, f32[16,8,128]{2,1,0:T(8,128)S(1)} %copy-done.11, f32[3,128,128]{2,1,0:T(8,128)S(1)} %copy-done.6, f32[3,128,128]{2,1,0:T(8,128)S(1)} %copy-done.8, ...), custom_call_target="tpu_custom_call" | custom-call | tf_op jit(solution)/shard_map/snr/pallas_call | solution.py:508
  (18 shorter events, 0.0 us)
Async XLA Ops:
  17.9 1.4 copy-start
  19.3 1.2 copy-start.1
  20.5 1.0 copy-start.3
  21.5 0.8 copy-start.12
  22.3 0.8 copy-start.13
  36.0 0.9 copy-start.2
  36.9 0.6 copy-start.14
  37.5 7.2 %copy-start.15 = (s32[2,15]{1,0:T(2,128)S(1)}, s32[2,15]{1,0:T(2,128)}, u32[]{:S(2)}) copy-start(s32[2,15]{1,0:T(2,128)} %edges.1) | copy-start | bytes 364
  37.5 99.6 %copy-start.4 = (bf16[256,512]{1,0:T(8,128)(2,1)S(1)}, bf16[256,512]{1,0:T(8,128)(2,1)}, u32[]{:S(2)}) copy-start(bf16[256,512]{1,0:T(8,128)(2,1)} %constant.76.clone.dft_hh) | copy-start | bytes 786436
  37.5 99.6 %copy-start.9 = (bf16[256,256]{1,0:T(8,128)(2,1)S(1)}, bf16[256,256]{1,0:T(8,128)(2,1)}, u32[]{:S(2)}) copy-start(bf16[256,256]{1,0:T(8,128)(2,1)} %constant.77.clone.dft_l) | copy-start | bytes 393220
  37.5 131.7 %all-to-all-start = ((f32[16,384,128]{2,1,0:T(8,128)}), f32[16,384,128]{2,1,0:T(8,128)S(1)}, u32[]{:S(2)}, u32[]{:S(2)}) async-start(f32[16,384,128]{2,1,0:T(8,128)} %get-tuple-element.7), calls=%async_computation | async-start | bytes 6291456 | tf_op jit(solution)/shard_map/all_to_all | solution.py:581
  137.1 0.9 copy-start.5
  138.0 0.9 copy-start.7
  138.9 0.8 copy-start.10
  139.8 0.7 copy-start.16
  140.5 0.7 copy-start.17
  169.2 0.9 copy-start.6
  170.1 0.9 copy-start.8
  171.0 0.8 copy-start.11

commit v2 on v0

v2 whole, which is shorter than its diff:
```python
import math

import jax
import jax.numpy as jnp
import numpy as np
from jax import lax
from jax.experimental import pallas as pl
from jax.experimental.pallas import tpu as pltpu
from jax.sharding import PartitionSpec as P

N1 = 2048
N2 = 512
DET = 3
NBLK = 32
BINS = 16
BF = jnp.bfloat16
F32 = jnp.float32
ANY = pl.BlockSpec(memory_space=pl.ANY)
SMEM = pl.BlockSpec(memory_space=pltpu.SMEM)
MESH = pl.DeviceIdType.MESH


def split(value):
    high = value.astype(BF)
    return high, (value - high.astype(F32)).astype(BF)


def radix4(x):
    (ar, ai), (br, bi), (cr, ci), (dr, di) = x
    pr, pi, mr, mi = ar + cr, ai + ci, ar - cr, ai - ci
    sr, si, tr, ti = br + dr, bi + di, br - dr, bi - di
    return [(pr + sr, pi + si), (mr - ti, mi + tr), (pr - sr, pi - si), (mr + ti, mi - tr)]


def times(x, c, s):
    return x[0] * c - x[1] * s, x[0] * s + x[1] * c


def radix16(x):
    mid = [radix4([x[low + 4 * high] for high in range(4)]) for low in range(4)]
    out = [None] * 16
    for first in range(4):
        row = []
        for low in range(4):
            angle = 2.0 * math.pi * low * first / 16
            value = mid[low][first]
            row.append(value if low * first == 0 else times(value, math.cos(angle), math.sin(angle)))
        for second, value in enumerate(radix4(row)):
            out[first + 4 * second] = value
    return out


def second_section(load, turn_c, turn_s, dft_hh, dft_l, stage_hl):
    @pl.loop(0, 8)
    def _(chunk):
        halves = []
        for sub in range(2):
            row = pl.multiple_of(chunk * 16 + sub * 8, 8)
            result = radix4([load(a, row) for a in range(4)])
            here = pl.ds(row, 8)
            for q in range(1, 4):
                result[q] = times(result[q], turn_c[q - 1, here, :], turn_s[q - 1, here, :])
            halves.append(result)
        row16 = pl.multiple_of(chunk * 16, 16)
        for q in range(4):
            for part in range(2):
                value = jnp.concatenate([halves[0][q][part], halves[1][q][part]], axis=0)
                high, low = split(value)
                lanes = slice(128 * q, 128 * q + 128)
                stage_hl[pl.ds(row16 + 128 * part, 16), lanes] = high
                stage_hl[pl.ds(row16 + 256 + 128 * part, 16), lanes] = low

    return jnp.dot(dft_hh[...], stage_hl[...], preferred_element_type=F32) + jnp.dot(
        dft_l[...], stage_hl[0:256, :], preferred_element_type=F32
    )


def sum_power(power):
    total = power[0]
    for f in range(1, 16):
        total = total + power[f]
    return total


def power_maps():
    col = lax.broadcasted_iota(jnp.int32, (8, 128), 1)
    row = lax.broadcasted_iota(jnp.int32, (8, 128), 0)
    block = 2 * (row + 8 * (lax.rem(col, 4) // 2)) + lax.rem(col, 2)
    return block, col // 4


def main_kernel(
    tmpl_pick, det_pick, edges, strain_hbm, tmpl_hbm, spin_hbm, send_twist_hbm, own_twist_hbm,
    base_hbm, step_hbm, turn_hbm, dft3_hbm, dft_hh_hbm, dft_l_hbm,
    arrived, power_all, chi_out,
    strain, tmpl, spin, send_twist, own_twist, base, step, turn, dft3, dft_hh, dft_l,
    gathered, sections, turned, outgoing, stage_hl, total, weight_s, order,
    table_sem, bank_send, bank_recv, freq_send, freq_recv, all_send, all_recv, local,
):
    here_b = lax.axis_index("bank")
    me = lax.axis_index("freq")
    z, core = here_b // 2, lax.rem(here_b, 2)
    my, mx = me // 4, lax.rem(me, 4)
    up = lax.rem(z + 1, 4) * 2 + core
    down = lax.rem(z + 3, 4) * 2 + core
    far = lax.rem(z + 2, 4) * 2 + core
    twin = z * 2 + 1 - core

    tables = [
        pltpu.make_async_copy(src, dst, table_sem.at[i])
        for i, (src, dst) in enumerate(
            [
                (tmpl_hbm, tmpl), (spin_hbm, spin), (send_twist_hbm, send_twist),
                (own_twist_hbm, own_twist), (base_hbm, base), (step_hbm, step),
                (turn_hbm, turn), (dft3_hbm, dft3), (dft_hh_hbm, dft_hh), (dft_l_hbm, dft_l),
                (strain_hbm, strain.at[here_b]),
            ]
        )
    ]
    for copy in tables:
        copy.start()

    barrier = pltpu.get_barrier_semaphore()
    for peer in (up, down, twin):
        pl.semaphore_signal(barrier, inc=1, device_id={"bank": peer}, device_id_type=MESH)
    for k in range(1, 16):
        pl.semaphore_signal(
            barrier, inc=1, device_id={"freq": lax.rem(me + k, 16)}, device_id_type=MESH
        )
    pl.semaphore_wait(barrier, 18)

    bank_sent = []

    def piece(owner, k):
        return strain.at[owner, pl.ds(3 * k, 3)]

    def pass_on(owner, k, peer, first=False):
        copy = pltpu.make_async_remote_copy(
            src_ref=strain_hbm.at[pl.ds(3 * k, 3)] if first else piece(owner, k),
            dst_ref=piece(owner, k),
            send_sem=bank_send.at[len(bank_sent)],
            recv_sem=bank_recv.at[owner, k],
            device_id={"bank": peer},
            device_id_type=MESH,
        )
        copy.start()
        bank_sent.append(copy)

    def landed(owner, k):
        pltpu.make_async_copy(piece(owner, k), piece(owner, k), bank_recv.at[owner, k]).wait()

    for k in range(2):
        pass_on(here_b, k, twin, True)
    for k in range(2):
        pass_on(here_b, k, up if k == 0 else down, True)
    for k in range(2):
        pass_on(here_b, k, down if k == 0 else up, True)

    def place(axis, along, across):
        dx, dy = (along, across) if axis == "x" else (across, along)
        return lax.rem(my + dy + 4, 4) * 4 + lax.rem(mx + dx + 4, 4)

    plans = [("x", "y", 1), ("y", "x", 1), ("x", "y", -1), ("y", "x", -1), ("x", "y", 1)]
    quarters = [z, lax.rem(z + 1, 4), lax.rem(z + 3, 4), lax.rem(z + 2, 4)]
    freq_sent = []
    counts = [0] * 5

    def part(p, owner):
        return power_all.at[owner] if p == 4 else gathered.at[owner, quarters[p]]

    def go(p, owner, axis, off):
        copy = pltpu.make_async_remote_copy(
            src_ref=part(p, owner),
            dst_ref=part(p, owner),
            send_sem=freq_send.at[p, counts[p]],
            recv_sem=freq_recv.at[p, owner],
            device_id={"freq": place(axis, off, 0)},
            device_id_type=MESH,
        )
        counts[p] += 1
        copy.start()
        freq_sent.append(copy)

    def came(p, owner):
        pltpu.make_async_copy(part(p, owner), part(p, owner), freq_recv.at[p, owner]).wait()

    def begin(p):
        first, second, s = plans[p]
        go(p, me, first, s)
        go(p, me, first, -s)
        go(p, me, second, s)
        go(p, me, second, -s)

    def near(p):
        first, second, s = plans[p]
        owner = place(first, -s, 0)
        came(p, owner)
        go(p, owner, first, s)
        go(p, owner, second, s)
        go(p, owner, second, -s)

    def other(p):
        first, second, s = plans[p]
        owner = place(first, s, 0)
        came(p, owner)
        go(p, owner, second, s)
        go(p, owner, second, -s)

    def cross(p, along):
        first, second, s = plans[p]
        owner = place(first, along * s, -s)
        came(p, owner)
        go(p, owner, second, s)

    def distant(p):
        first, second, s = plans[p]
        owner = place(first, 2, 0)
        came(p, owner)
        go(p, owner, second, s)
        go(p, owner, second, -s)

    tables[0].wait()
    col = lax.broadcasted_iota(jnp.int32, (128, 128), 1)
    depth = lax.broadcasted_iota(jnp.int32, (128, 128), 0)
    own_power = jnp.zeros((8, 128), F32)
    for t in range(2):
        for g in range(2):
            sums = []
            for a in range(8 * g, 8 * g + 8):
                lanes = pl.ds(a * 128, 128)
                hr, hi = tmpl[t, 0, :, lanes], tmpl[t, 1, :, lanes]
                sums.append(jnp.sum(hr * hr + hi * hi, axis=0, keepdims=True))
            select = (col == 4 * t + 2 * g + depth // 64).astype(F32)
            own_power += jnp.dot(
                jnp.concatenate(sums, axis=0),
                select,
                precision=lax.Precision.HIGHEST,
                preferred_element_type=F32,
            )
    power_all[me] = own_power
    begin(4)

    t_pick = tmpl_pick[0]
    d_pick = det_pick[0]
    left = lax.broadcasted_iota(jnp.int32, (8, 128), 1) < 64

    def entry(quarter):
        @pl.loop(0, 4)
        def _(chunk):
            rows = pl.ds(pl.multiple_of(chunk * 8, 8), 8)
            for sub in range(4):
                lanes = pl.ds(pl.multiple_of(quarter * 512 + sub * 128, 128), 128)
                half = slice((sub % 2) * 128, (sub % 2) * 128 + 128)
                who = quarter * 2 + sub // 2
                hr, hi = tmpl[t_pick, 0, rows, lanes], tmpl[t_pick, 1, rows, lanes]
                sr, si = [
                    jnp.where(
                        d_pick == 0,
                        strain[who, k, rows, half],
                        jnp.where(
                            d_pick == 1, strain[who, 2 + k, rows, half], strain[who, 4 + k, rows, half]
                        ),
                    )
                    for k in range(2)
                ]
                re, im = hr * sr + hi * si, hr * si - hi * sr
                re_far, im_far = pltpu.roll(re, 64, 1), pltpu.roll(im, 64, 1)
                gathered[me, quarter, rows, 256 * sub : 256 * sub + 128] = jnp.where(left, re, im_far)
                gathered[me, quarter, rows, 256 * sub + 128 : 256 * sub + 256] = jnp.where(
                    left, re_far, im
                )

    tables[10].wait()
    for k in range(2):
        landed(twin, k)
    entry(quarters[0])
    begin(0)
    landed(down, 0)
    pass_on(down, 0, up)
    pass_on(down, 0, twin)
    landed(up, 1)
    pass_on(up, 1, down)
    pass_on(up, 1, twin)
    landed(up, 0)
    pass_on(up, 0, twin)
    landed(down, 1)
    pass_on(down, 1, twin)
    near(0)
    other(0)
    near(4)
    other(4)
    for p, step_z in ((1, 1), (2, 3)):
        for k in range(2):
            landed(lax.rem(z + step_z, 4) * 2 + 1 - core, k)
        entry(quarters[p])
        begin(p)
    for k in range(2):
        landed(far, k)
        pass_on(far, k, twin)
    for k in range(2):
        landed(lax.rem(z + 2, 4) * 2 + 1 - core, k)
    entry(quarters[3])
    begin(3)

    tables[1].wait()

    def radix_steps(low, high):
        @pl.loop(low, high)
        def _(index):
            series = index // 4
            t, d = series // 3, lax.rem(series, 3)
            rows = pl.ds(pl.multiple_of(lax.rem(index, 4) * 8, 8), 8)
            where = lax.rem(index, 4) * 8 + series * 32
            values = []
            for a in range(16):
                half = slice((a % 2) * 128, (a % 2) * 128 + 128)
                lanes = pl.ds(a * 128, 128)
                hr, hi = tmpl[t, 0, rows, lanes], tmpl[t, 1, rows, lanes]
                sr, si = strain[a // 2, 2 * d, rows, half], strain[a // 2, 2 * d + 1, rows, half]
                values.append((hr * sr + hi * si, hr * si - hi * sr))
            result = radix16(values)
            for q in range(16):
                re, im = result[q]
                if q:
                    re, im = times((re, im), spin[0, q], spin[1, q])
                here = pl.ds(pl.multiple_of((q % 2) * 256 + where, 8), 8)
                sections[q // 2, here, 0:128] = re
                sections[q // 2, here, 128:256] = im

    def line_steps(low, high):
        @pl.loop(low, high)
        def _(q):
            start = pl.multiple_of(lax.rem(q, 2) * 256, 256)
            high_part, low_part = split(sections[q // 2, pl.ds(start, 256), :])
            stack = jnp.concatenate([high_part, low_part, high_part], axis=1)
            out = lax.dot_general(
                dft3[...], stack, (((1,), (1,)), ((), ())), preferred_element_type=F32
            )
            for half in range(2):
                for h in range(2):
                    turned[half, h, pl.ds(q, 128, stride=16), :] = out[
                        half * 128 : half * 128 + 128, h * 128 : h * 128 + 128
                    ]

    def turn_steps(low, high):
        @pl.loop(low, high)
        def _(f):
            here = pl.ds(pl.multiple_of(f * 128, 128), 128)
            c, s = send_twist[0, :, here], send_twist[1, :, here]
            for h in range(2):
                re = turned[0, h, here, :].T
                im = turned[1, h, here, :].T
                for k in range(4 - 2 * h):
                    rows = slice(32 * k, 32 * k + 32)
                    out_re, out_im = times((re[rows], im[rows]), c, s)
                    top = 128 * h + 32 * k
                    outgoing[f, top : top + 32, :] = out_re
                    outgoing[f, 192 + top : 192 + top + 32, :] = out_im

    for q in range(16):
        sections[q // 2, (q % 2) * 256 + 192 : (q % 2) * 256 + 256, :] = jnp.zeros((64, 256), F32)
    radix_steps(0, 12)
    near(1)
    near(2)
    radix_steps(12, 24)
    tables[7].wait()
    near(3)
    for p in (1, 2, 3):
        other(p)
    line_steps(0, 8)
    for p in (0, 4, 1, 2):
        cross(p, 0)
    line_steps(8, 16)
    tables[2].wait()
    cross(3, 0)
    for p in (0, 4, 1, 2, 3):
        distant(p)
    turn_steps(0, 8)
    for p in (0, 4, 1, 2, 3):
        cross(p, -1)
    turn_steps(8, 16)
    for along in (1, 2):
        for p in (0, 4, 1, 2, 3):
            cross(p, along)

    keep = pltpu.make_async_copy(outgoing.at[me], arrived.at[me], local)
    keep.start()
    all_sent = []
    for i, k in enumerate((10, 9, 11, 6, 14, 7, 13, 5, 15, 3, 8, 2, 12, 4, 1)):
        peer = lax.rem(me + k, 16)
        copy = pltpu.make_async_remote_copy(
            src_ref=outgoing.at[peer],
            dst_ref=arrived.at[me],
            send_sem=all_send.at[k - 1],
            recv_sem=all_recv.at[k - 1],
            device_id={"freq": peer},
            device_id_type=MESH,
        )
        copy.start()
        all_sent.append(copy)

    for along in (0, -1, 1, 2):
        for across in (1, 2):
            for p, (first, second, s) in enumerate(plans):
                came(p, place(first, along * s, across * s))

    for i in (3, 4, 5, 6, 8, 9):
        tables[i].wait()
    block, owner = power_maps()
    mine = jnp.where(owner == t_pick, sum_power(power_all), 0.0)
    sigma_sq = jnp.sum(mine, keepdims=True)
    for level in range(BINS):
        low = 0 if level == 0 else edges[t_pick, level - 1]
        high = NBLK if level == BINS - 1 else edges[t_pick, level]
        inside = (block >= low) & (block < high)
        bin_power = jnp.sum(jnp.where(inside, mine, 0.0), keepdims=True)
        weight_s[level] = jnp.broadcast_to(bin_power / sigma_sq, (8, 128))

    @pl.loop(0, NBLK)
    def _(b):
        pc, ps = step[0, pl.ds(b, 1), :], step[1, pl.ds(b, 1), :]
        wr, wi = times((base[0], base[1]), pc, ps)
        matrix = jnp.concatenate(
            [jnp.concatenate([wr, wi], axis=1), jnp.concatenate([-wi, wr], axis=1)], axis=0
        )
        m_high, m_low = split(matrix)
        lanes = pl.ds(pl.multiple_of(lax.rem(b, 8) * 128, 128), 128)
        high, low = split(gathered[:, b // 8, :, lanes].reshape(N2, 128))
        section = jnp.dot(
            jnp.concatenate([high, low], axis=1),
            jnp.concatenate([m_high, m_high], axis=0),
            preferred_element_type=F32,
        ) + jnp.dot(high, m_low, preferred_element_type=F32)
        fresh = b == 0
        for level in range(BINS - 1):
            fresh = fresh | (edges[t_pick, level] == b)
        before = sections[jnp.maximum(b - 1, 0)]
        sections[b] = section + jnp.where(fresh, 0.0, before)

    total[...] = jnp.zeros((256, N2), F32)

    @pl.loop(0, BINS)
    def _(level):
        edge = edges[t_pick, jnp.minimum(level, BINS - 2)]
        last = jnp.clip(jnp.where(level == BINS - 1, NBLK, edge) - 1, 0, NBLK - 1)

        def load(a, row):
            here = pl.ds(a * 128 + row, 8)
            value = (sections[last, here, 0:128], sections[last, here, 128:256])
            return times(value, own_twist[0, here, :], own_twist[1, here, :])

        result = second_section(load, turn.at[0], turn.at[1], dft_hh, dft_l, stage_hl)
        sections[level, 0:256, :] = result[:, 0:256]
        sections[level, 256:512, :] = result[:, 256:512]
        total[...] += result

    inv = 1.0 / sigma_sq

    @pl.loop(0, 16)
    def _(chunk):
        row = pl.multiple_of(chunk * 8, 8)
        for q in range(4):
            whole_lanes = slice(128 * q, 128 * q + 128)
            lanes = slice(128 * (q % 2), 128 * (q % 2) + 128)
            whole_re = total[pl.ds(row, 8), whole_lanes]
            whole_im = total[pl.ds(128 + row, 8), whole_lanes]
            sums = jnp.zeros((8, 128), F32)
            for level in range(BINS):
                weight = weight_s[level]
                top = 256 * (q // 2) + row
                dev_re = sections[level, pl.ds(top, 8), lanes] - weight * whole_re
                dev_im = sections[level, pl.ds(top + 128, 8), lanes] - weight * whole_im
                sums += (dev_re * dev_re + dev_im * dev_im) * (1.0 / weight)
            order[pl.ds(q + 4 * row, 8, stride=4), :] = sums * inv

    chi_out[0] = order[...].T

    for k in range(1, 16):
        source = lax.rem(me + 16 - k, 16)
        pltpu.make_async_copy(arrived.at[source], arrived.at[source], all_recv.at[k - 1]).wait()
    keep.wait()
    for copy in bank_sent + freq_sent + all_sent:
        copy.wait_send()


def main_call(tmpl_pick, det_pick, edges, strain, tmpl, *tables):
    vmem = pl.BlockSpec(memory_space=pltpu.VMEM)
    shapes = [
        pltpu.VMEM((8,) + strain.shape, F32),
        pltpu.VMEM(tmpl.shape, F32),
    ] + [pltpu.VMEM(v.shape, v.dtype) for v in tables]
    return pl.pallas_call(
        main_kernel,
        out_shape=(
            jax.ShapeDtypeStruct((16, 384, 128), F32),
            jax.ShapeDtypeStruct((16, 8, 128), F32),
            jax.ShapeDtypeStruct((1, 128, N2), F32),
        ),
        in_specs=[SMEM] * 3 + [ANY] * (2 + len(tables)),
        out_specs=(ANY, vmem, vmem),
        scratch_shapes=shapes
        + [
            pltpu.VMEM((16, 4, 32, 1024), F32),
            pltpu.VMEM((NBLK, N2, 256), F32),
            pltpu.VMEM((2, 2, N1, 128), F32),
            pltpu.VMEM((16, 384, 128), F32),
            pltpu.VMEM((512, N2), BF),
            pltpu.VMEM((256, N2), F32),
            pltpu.VMEM((BINS, 8, 128), F32),
            pltpu.VMEM((N2, 128), F32),
            pltpu.SemaphoreType.DMA((11,)),
            pltpu.SemaphoreType.DMA((14,)),
            pltpu.SemaphoreType.DMA((8, 2)),
            pltpu.SemaphoreType.DMA((5, 15)),
            pltpu.SemaphoreType.DMA((5, 16)),
            pltpu.SemaphoreType.DMA((15,)),
            pltpu.SemaphoreType.DMA((15,)),
            pltpu.SemaphoreType.DMA,
        ],
        compiler_params=pltpu.CompilerParams(
            collective_id=1, has_side_effects=True, vmem_limit_bytes=56 << 20
        ),
        name="main",
    )(tmpl_pick, det_pick, edges, strain, tmpl, *tables)


def snr_kernel(in_re, in_im, power, turn_c, turn_s, dft_hh, dft_l, out, stage_hl, order):
    t = pl.program_id(0) // DET
    _, owner = power_maps()
    sigma_sq = jnp.sum(jnp.where(owner == t, sum_power(power), 0.0), keepdims=True)
    inv = 1.0 / jnp.sqrt(sigma_sq)

    def load(a, row):
        source = 4 * a + row // 32
        here = pl.ds(lax.rem(row, 32), 8)
        return in_re[source, here, :], in_im[source, here, :]

    result = second_section(load, turn_c, turn_s, dft_hh, dft_l, stage_hl) * inv
    for part in range(2):
        for q in range(4):
            order[pl.ds(q, 128, stride=4), :] = result[
                part * 128 : part * 128 + 128, q * 128 : q * 128 + 128
            ]
        out[0, 0, part] = order[...].T


def snr_of(arrived, power, turn, dft_hh, dft_l):
    whole = lambda *shape: pl.BlockSpec(shape, lambda i: (0,) * len(shape))
    return pl.pallas_call(
        snr_kernel,
        out_shape=jax.ShapeDtypeStruct((2, DET, 2, 128, N2), F32),
        grid=(6,),
        in_specs=[
            pl.BlockSpec((16, 32, 128), lambda i: (0, i, 0)),
            pl.BlockSpec((16, 32, 128), lambda i: (0, i + 6, 0)),
            whole(16, 8, 128),
            whole(3, 128, 128),
            whole(3, 128, 128),
            whole(256, 512),
            whole(256, 256),
        ],
        out_specs=pl.BlockSpec((1, 1, 2, 128, N2), lambda i: (i // DET, lax.rem(i, DET), 0, 0, 0)),
        scratch_shapes=[pltpu.VMEM((512, N2), BF), pltpu.VMEM((N2, 128), F32)],
        compiler_params=pltpu.CompilerParams(vmem_limit_bytes=32 << 20),
        name="snr",
    )(arrived, arrived, power, *turn, dft_hh, dft_l)


def turns(product, length):
    angle = (product % length).astype(F32) * (2.0 * math.pi / length)
    return jnp.cos(angle), jnp.sin(angle)


def fixed_turns(product, length):
    angle = 2.0 * np.pi * (product % length) / length
    return np.cos(angle), np.sin(angle)


def fixed_tables():
    index = np.arange(128)
    c, s = fixed_turns(index[:, None] * index[None, :], 128)
    full = np.concatenate(
        [np.concatenate([c, -s], axis=1), np.concatenate([s, c], axis=1)], axis=0
    ).astype(np.float32)
    high = full.astype(jnp.bfloat16)
    low = (full - high.astype(np.float32)).astype(jnp.bfloat16)
    spin = [
        np.ascontiguousarray(np.broadcast_to(v[:, None, :], (16, 8, 128))).astype(np.float32)
        for v in fixed_turns(np.arange(16)[:, None] * index[None, :], N1)
    ]
    turn = [
        np.ascontiguousarray(np.broadcast_to(v[:, :, None], (3, 128, 128))).astype(np.float32)
        for v in fixed_turns(np.arange(1, 4)[:, None] * index[None, :], N2)
    ]
    step = [
        v.astype(np.float32)
        for v in fixed_turns(np.arange(NBLK)[:, None] * index[None, :], NBLK)
    ]
    return high, low, spin, turn, step


def per_device(strain, templates, coinc_tmpl, coinc_det, bin_edges):
    high, low, spin, turn, step = fixed_tables()
    dft3 = np.concatenate([high, high, low], axis=1)
    dft_hh = np.concatenate([high, high], axis=1)
    place = lax.axis_index("freq")
    rows = place * 32 + jnp.arange(32, dtype=jnp.int32)
    times_all = jnp.arange(N1, dtype=jnp.int32)
    times_own = place * 128 + jnp.arange(128, dtype=jnp.int32)
    send_twist = turns(rows[:, None] * times_all[None, :], N1 * N2)
    own_twist = turns(jnp.arange(N2, dtype=jnp.int32)[:, None] * times_own[None, :], N1 * N2)
    base = turns(jnp.arange(64, dtype=jnp.int32)[:, None] * times_own[None, :], N1)
    arrived, power_all, chi_sq = main_call(
        coinc_tmpl, coinc_det, bin_edges, strain.reshape(2 * DET, 32, 256), templates,
        np.stack(spin), jnp.stack(send_twist), jnp.stack(own_twist), jnp.stack(base),
        np.stack(step), np.stack(turn), dft3, dft_hh, low,
    )
    snr = snr_of(arrived, power_all, turn, dft_hh, low)
    return (snr, chi_sq)


def solution(mesh):
    placed = (
        P(None, None, "freq", "bank"),
        P("bank", None, "freq", None),
        P("bank"),
        P("bank"),
        P("bank", None),
    )
    return jax.shard_map(
        per_device,
        mesh=mesh,
        in_specs=placed,
        out_specs=(P("bank", None, None, "freq", None), P("bank", "freq", None)),
        check_vma=False,
    )
```

time: 1110 us -> 128 us (0.12)
  the two profiles are of different devices: /device:TPU:0 before, /device:TPU:30 now
where the time goes in v2:
time: 128 us; the launch traced here: 127 us
  Pallas kernels  117 us (91%)
  other arithmetic  4.6 us (4%)
  local copies, waits for them, and re-layouts  3.46 us (3%)
  between operations  2.03 us (2%)
    pallas_call x1, Pallas kernels, main_call(): pl.pallas_call(main_kernel, out_shape=(jax.ShapeDtypeStruct((16, 384, 128...  110 us
    pallas_call x1, Pallas kernels, snr_of(): pl.pallas_call(snr_kernel, out_shape=jax.ShapeDtypeStruct((2, DET, 2, 128...  7 us
    unnamed x15, local copies, waits for them, and re-layouts  3.46 us

profile of v2, /device:TPU:30, one launch (start us, length us, event | category | flops | bytes accessed | tf_op | source)
XLA Modules:
  0.0 127.3 jit_solution(12603686037837484237)
XLA Ops:
  1.9 0.1 fusion.23
  2.1 0.6 pad_maximum_fusion.2.base_hbm
  2.7 1.0 fusion.13
  3.8 0.0 copy-start.1
  3.8 0.0 copy-start.2
  3.8 0.0 copy-start.3
  3.8 0.0 copy-start.4
  3.8 0.8 pad_maximum_fusion.1.own_twist_hbm
  4.7 1.1 fusion.15
  5.8 0.8 pad_maximum_fusion.send_twist_hbm
  6.6 110.2 %main.1 = (f32[16,384,128]{2,1,0:T(8,128)}, f32[16,8,128]{2,1,0:T(8,128)}, f32[1,128,512]{2,1,0:T(8,128)}) custom-call(s32[1]{0:T(128)S(6)} %copy.16.tmpl_pick, s32[1]{0:T(128)S(6)} %copy.17.det_pick, s32[2,15]{1,0:T(2,128)} %edges.1, f32[6,32,256]{2,1,0:T(8,128)} %bitcast.1, f32[2,2,32,2048]{3,2,1,0:T(8,128)} %tmpl_hbm.1, ...), custom_call_target="tpu_custom_call" | custom-call | tf_op jit(solution)/shard_map/main/pallas_call | solution.py:492
  116.8 0.0 copy-done.1
  116.8 0.0 copy-done.2
  116.8 0.0 copy-done.3
  116.8 0.0 copy-done.4
  116.9 0.0 copy-start
  116.9 1.9 %copy-done = f32[16,384,128]{2,1,0:T(8,128)S(1)} copy-done((f32[16,384,128]{2,1,0:T(8,128)S(1)}, f32[16,384,128]{2,1,0:T(8,128)}, u32[]{:S(2)}) %copy-start) | copy-done | bytes 3145752
  118.8 0.0 copy-start.5
  118.8 0.8 copy-done.5
  119.6 0.0 copy-start.6
  119.6 7.0 %snr.1 = f32[2,3,2,128,512]{4,3,2,1,0:T(8,128)} custom-call(f32[16,384,128]{2,1,0:T(8,128)S(1)} %copy-done, f32[16,384,128]{2,1,0:T(8,128)S(1)} %copy-done, f32[16,8,128]{2,1,0:T(8,128)S(1)} %copy-done.5, f32[3,128,128]{2,1,0:T(8,128)S(1)} %copy-done.4, f32[3,128,128]{2,1,0:T(8,128)S(1)} %copy-done.3, bf16[256,512]{1,0:T(8,128)(2,1)S(1)} %copy-done.1, ...), custom_call_target="tpu_custom_call" | custom-call | tf_op jit(solution)/shard_map/snr/pallas_call | solution.py:549
  126.6 0.0 copy-done.6
  126.6 0.7 copy.18
  (2 shorter events, 0.0 us)
Async XLA Ops:
  3.8 113.0 %copy-start.1 = (bf16[256,512]{1,0:T(8,128)(2,1)S(1)}, bf16[256,512]{1,0:T(8,128)(2,1)}, u32[]{:S(2)}) copy-start(bf16[256,512]{1,0:T(8,128)(2,1)} %constant.70.clone.dft_hh_hbm.dft_hh) | copy-start | bytes 786436
  3.8 113.0 %copy-start.2 = (bf16[256,256]{1,0:T(8,128)(2,1)S(1)}, bf16[256,256]{1,0:T(8,128)(2,1)}, u32[]{:S(2)}) copy-start(bf16[256,256]{1,0:T(8,128)(2,1)} %constant.71.clone.dft_l_hbm.dft_l) | copy-start | bytes 393220
  3.8 113.0 %copy-start.3 = (f32[3,128,128]{2,1,0:T(8,128)S(1)}, f32[3,128,128]{2,1,0:T(8,128)}, u32[]{:S(2)}) copy-start(f32[3,128,128]{2,1,0:T(8,128)} %constant.73.clone.turn_s) | copy-start | bytes 589828
  3.8 113.0 %copy-start.4 = (f32[3,128,128]{2,1,0:T(8,128)S(1)}, f32[3,128,128]{2,1,0:T(8,128)}, u32[]{:S(2)}) copy-start(f32[3,128,128]{2,1,0:T(8,128)} %constant.72.clone.turn_c) | copy-start | bytes 589828
  116.9 1.9 %copy-start = (f32[16,384,128]{2,1,0:T(8,128)S(1)}, f32[16,384,128]{2,1,0:T(8,128)}, u32[]{:S(2)}) copy-start(f32[16,384,128]{2,1,0:T(8,128)} %get-tuple-element.5.in_re.in_im) | copy-start | bytes 9437188
  118.8 0.8 copy-start.5
  119.6 7.0 %copy-start.6 = (f32[1,128,512]{2,1,0:T(8,128)S(1)}, f32[1,128,512]{2,1,0:T(8,128)}, u32[]{:S(2)}) copy-start(f32[1,128,512]{2,1,0:T(8,128)} %get-tuple-element.17) | copy-start | bytes 786436

commit v3 on v2

--- a/solution.py
+++ b/solution.py
@@ -50,7 +50,7 @@
     return out
 
 
-def second_section(load, turn_c, turn_s, dft_hh, dft_l, stage_hl):
+def second_section(load, turn, dft, stage_hl):
     @pl.loop(0, 8)
     def _(chunk):
         halves = []
@@ -59,7 +59,7 @@
             result = radix4([load(a, row) for a in range(4)])
             here = pl.ds(row, 8)
             for q in range(1, 4):
-                result[q] = times(result[q], turn_c[q - 1, here, :], turn_s[q - 1, here, :])
+                result[q] = times(result[q], turn[0, q - 1, here, :], turn[1, q - 1, here, :])
             halves.append(result)
         row16 = pl.multiple_of(chunk * 16, 16)
         for q in range(4):
@@ -70,8 +70,8 @@
                 stage_hl[pl.ds(row16 + 128 * part, 16), lanes] = high
                 stage_hl[pl.ds(row16 + 256 + 128 * part, 16), lanes] = low
 
-    return jnp.dot(dft_hh[...], stage_hl[...], preferred_element_type=F32) + jnp.dot(
-        dft_l[...], stage_hl[0:256, :], preferred_element_type=F32
+    return jnp.dot(dft[:, 0:512], stage_hl[...], preferred_element_type=F32) + jnp.dot(
+        dft[:, 512:768], stage_hl[0:256, :], preferred_element_type=F32
     )
 
 
@@ -90,11 +90,10 @@
 
 
 def main_kernel(
-    tmpl_pick, det_pick, edges, strain_hbm, tmpl_hbm, spin_hbm, send_twist_hbm, own_twist_hbm,
-    base_hbm, step_hbm, turn_hbm, dft3_hbm, dft_hh_hbm, dft_l_hbm,
-    arrived, power_all, chi_out,
-    strain, tmpl, spin, send_twist, own_twist, base, step, turn, dft3, dft_hh, dft_l,
-    gathered, sections, turned, outgoing, stage_hl, total, weight_s, order,
+    tmpl_pick, det_pick, edges, strain_hbm, tmpl_hbm, spin_hbm, fixed_hbm, row_hbm, step_hbm, turn_hbm, dft_hbm,
+    arrived, power_all, total, chi_out,
+    strain, tmpl, spin, fixed, row_turn, step, turn, dft,
+    gathered, sections, turned, outgoing, stage_hl, weight_s, order, own_twist, base,
     table_sem, bank_send, bank_recv, freq_send, freq_recv, all_send, all_recv, local,
 ):
     here_b = lax.axis_index("bank")
@@ -110,10 +109,9 @@
         pltpu.make_async_copy(src, dst, table_sem.at[i])
         for i, (src, dst) in enumerate(
             [
-                (tmpl_hbm, tmpl), (spin_hbm, spin), (send_twist_hbm, send_twist),
-                (own_twist_hbm, own_twist), (base_hbm, base), (step_hbm, step),
-                (turn_hbm, turn), (dft3_hbm, dft3), (dft_hh_hbm, dft_hh), (dft_l_hbm, dft_l),
-                (strain_hbm, strain.at[here_b]),
+                (tmpl_hbm, tmpl), (strain_hbm, strain.at[here_b]), (spin_hbm, spin),
+                (dft_hbm, dft), (fixed_hbm, fixed), (step_hbm, step), (turn_hbm, turn),
+                (row_hbm, row_turn),
             ]
         )
     ]
@@ -160,13 +158,16 @@
         dx, dy = (along, across) if axis == "x" else (across, along)
         return lax.rem(my + dy + 4, 4) * 4 + lax.rem(mx + dx + 4, 4)
 
-    plans = [("x", "y", 1), ("y", "x", 1), ("x", "y", -1), ("y", "x", -1), ("x", "y", 1)]
+    plans = [("x", "y", 1), ("y", "x", -1), ("x", "y", -1), ("y", "x", 1)] * 2 + [("x", "y", 1)]
+    small = 8
     quarters = [z, lax.rem(z + 1, 4), lax.rem(z + 3, 4), lax.rem(z + 2, 4)]
     freq_sent = []
-    counts = [0] * 5
+    counts = [0] * 9
 
     def part(p, owner):
-        return power_all.at[owner] if p == 4 else gathered.at[owner, quarters[p]]
+        if p == small:
+            return power_all.at[owner]
+        return gathered.at[owner, quarters[p // 2], pl.ds(16 * (p % 2), 16)]
 
     def go(p, owner, axis, off):
         copy = pltpu.make_async_remote_copy(
@@ -238,10 +239,11 @@
                 preferred_element_type=F32,
             )
     power_all[me] = own_power
-    begin(4)
+    begin(small)
 
     t_pick = tmpl_pick[0]
     d_pick = det_pick[0]
+    own_series = DET * t_pick + d_pick
     left = lax.broadcasted_iota(jnp.int32, (8, 128), 1) < 64
 
     def entry(quarter):
@@ -270,11 +272,16 @@
                     left, re_far, im
                 )
 
-    tables[10].wait()
+    def both(act, *pairs, along=None):
+        for i in pairs:
+            for p in (small,) if i == 4 else (2 * i, 2 * i + 1):
+                act(p) if along is None else act(p, along)
+
+    tables[1].wait()
     for k in range(2):
         landed(twin, k)
     entry(quarters[0])
-    begin(0)
+    both(begin, 0)
     landed(down, 0)
     pass_on(down, 0, up)
     pass_on(down, 0, twin)
@@ -285,24 +292,25 @@
     pass_on(up, 0, twin)
     landed(down, 1)
     pass_on(down, 1, twin)
-    near(0)
-    other(0)
-    near(4)
-    other(4)
-    for p, step_z in ((1, 1), (2, 3)):
+    both(near, 0)
+    both(other, 0)
+    for i, step_z in ((1, 1), (2, 3)):
         for k in range(2):
             landed(lax.rem(z + step_z, 4) * 2 + 1 - core, k)
-        entry(quarters[p])
-        begin(p)
+        entry(quarters[i])
+        both(begin, i)
+    both(near, 4)
+    both(other, 4)
+    both(cross, 0, along=0)
     for k in range(2):
         landed(far, k)
         pass_on(far, k, twin)
     for k in range(2):
         landed(lax.rem(z + 2, 4) * 2 + 1 - core, k)
     entry(quarters[3])
-    begin(3)
-
-    tables[1].wait()
+    both(begin, 3)
+
+    tables[2].wait()
 
     def radix_steps(low, high):
         @pl.loop(low, high)
@@ -334,7 +342,7 @@
             high_part, low_part = split(sections[q // 2, pl.ds(start, 256), :])
             stack = jnp.concatenate([high_part, low_part, high_part], axis=1)
             out = lax.dot_general(
-                dft3[...], stack, (((1,), (1,)), ((), ())), preferred_element_type=F32
+                dft[...], stack, (((1,), (1,)), ((), ())), preferred_element_type=F32
             )
             for half in range(2):
                 for h in range(2):
@@ -346,42 +354,88 @@
         @pl.loop(low, high)
         def _(f):
             here = pl.ds(pl.multiple_of(f * 128, 128), 128)
-            c, s = send_twist[0, :, here], send_twist[1, :, here]
+            row = pl.ds(f, 1)
+            c, s = times(
+                (fixed[0, 0:32, here], fixed[1, 0:32, here]),
+                row_turn[0, me, row, :],
+                row_turn[1, me, row, :],
+            )
+            series = []
             for h in range(2):
                 re = turned[0, h, here, :].T
                 im = turned[1, h, here, :].T
                 for k in range(4 - 2 * h):
-                    rows = slice(32 * k, 32 * k + 32)
-                    out_re, out_im = times((re[rows], im[rows]), c, s)
-                    top = 128 * h + 32 * k
-                    outgoing[f, top : top + 32, :] = out_re
-                    outgoing[f, 192 + top : 192 + top + 32, :] = out_im
+                    series.append((re[32 * k : 32 * k + 32], im[32 * k : 32 * k + 32]))
+            for slot in range(5):
+                value = [
+                    jnp.where(own_series <= slot, after, before)
+                    for before, after in zip(series[slot], series[slot + 1])
+                ]
+                out_re, out_im = times(value, c, s)
+                outgoing[f, 32 * slot : 32 * slot + 32, :] = out_re
+                outgoing[f, 160 + 32 * slot : 192 + 32 * slot, :] = out_im
 
     for q in range(16):
         sections[q // 2, (q % 2) * 256 + 192 : (q % 2) * 256 + 256, :] = jnp.zeros((64, 256), F32)
-    radix_steps(0, 12)
-    near(1)
-    near(2)
-    radix_steps(12, 24)
+    radix_steps(0, 6)
+    both(near, 1, 2)
+    radix_steps(6, 12)
+    both(other, 1, 2)
+    both(distant, 0, 4)
+    both(cross, 4, along=0)
+    radix_steps(12, 18)
+    both(cross, 0, 4, along=-1)
+    radix_steps(18, 24)
+    both(cross, 1, 2, along=0)
+    both(near, 3)
+    tables[3].wait()
+    line_steps(0, 4)
+    both(distant, 1, 2)
+    both(other, 3)
+    line_steps(4, 8)
+    both(cross, 0, 4, along=1)
+    line_steps(8, 12)
+    both(cross, 1, 2, along=-1)
+    line_steps(12, 16)
+    both(cross, 3, along=0)
+    both(cross, 0, 4, along=2)
+    tables[4].wait()
     tables[7].wait()
-    near(3)
-    for p in (1, 2, 3):
-        other(p)
-    line_steps(0, 8)
-    for p in (0, 4, 1, 2):
-        cross(p, 0)
-    line_steps(8, 16)
-    tables[2].wait()
-    cross(3, 0)
-    for p in (0, 4, 1, 2, 3):
-        distant(p)
-    turn_steps(0, 8)
-    for p in (0, 4, 1, 2, 3):
-        cross(p, -1)
-    turn_steps(8, 16)
-    for along in (1, 2):
-        for p in (0, 4, 1, 2, 3):
-            cross(p, along)
+    turn_steps(0, 4)
+    both(distant, 3)
+    both(cross, 1, 2, along=1)
+    turn_steps(4, 8)
+    both(cross, 3, along=-1)
+    turn_steps(8, 12)
+    both(cross, 1, 2, along=2)
+    turn_steps(12, 16)
+    both(cross, 3, along=1)
+
+    own_lanes = pl.ds(pl.multiple_of(me * 128, 128), 128)
+    for source in range(16):
+        row = pl.ds(me, 1)
+        out_c, out_s = times(
+            (fixed[0, 0:32, own_lanes], fixed[1, 0:32, own_lanes]),
+            row_turn[0, source, row, :],
+            row_turn[1, source, row, :],
+        )
+        own_twist[0, 32 * source : 32 * source + 32, :] = out_c
+        own_twist[1, 32 * source : 32 * source + 32, :] = out_s
+    for u in range(8):
+        row = slice(32 + u, 33 + u)
+        out_c, out_s = times(
+            (fixed[0, 40:48, own_lanes], fixed[1, 40:48, own_lanes]),
+            fixed[0, row, own_lanes],
+            fixed[1, row, own_lanes],
+        )
+        base[0, 8 * u : 8 * u + 8, :] = out_c
+        base[1, 8 * u : 8 * u + 8, :] = out_s
+    both(cross, 3, along=2)
+
+    for along in (0, -1, 1, 2):
+        for across in (1, 2):
+            for p, (first, second, s) in enumerate(plans):
+                came(p, place(first, along * s, across * s))
 
     keep = pltpu.make_async_copy(outgoing.at[me], arrived.at[me], local)
     keep.start()
@@ -399,12 +453,7 @@
         copy.start()
         all_sent.append(copy)
 
-    for along in (0, -1, 1, 2):
-        for across in (1, 2):
-            for p, (first, second, s) in enumerate(plans):
-                came(p, place(first, along * s, across * s))
-
-    for i in (3, 4, 5, 6, 8, 9):
+    for i in (5, 6):
         tables[i].wait()
     block, owner = power_maps()
     mine = jnp.where(owner == t_pick, sum_power(power_all), 0.0)
@@ -449,7 +498,7 @@
             value = (sections[last, here, 0:128], sections[last, here, 128:256])
             return times(value, own_twist[0, here, :], own_twist[1, here, :])
 
-        result = second_section(load, turn.at[0], turn.at[1], dft_hh, dft_l, stage_hl)
+        result = second_section(load, turn, dft, stage_hl)
         sections[level, 0:256, :] = result[:, 0:256]
         sections[level, 256:512, :] = result[:, 256:512]
         total[...] += result
@@ -492,27 +541,29 @@
     return pl.pallas_call(
         main_kernel,
         out_shape=(
-            jax.ShapeDtypeStruct((16, 384, 128), F32),
+            jax.ShapeDtypeStruct((16, 320, 128), F32),
             jax.ShapeDtypeStruct((16, 8, 128), F32),
+            jax.ShapeDtypeStruct((256, N2), F32),
             jax.ShapeDtypeStruct((1, 128, N2), F32),
         ),
         in_specs=[SMEM] * 3 + [ANY] * (2 + len(tables)),
-        out_specs=(ANY, vmem, vmem),
+        out_specs=(ANY, vmem, vmem, vmem),
         scratch_shapes=shapes
         + [
             pltpu.VMEM((16, 4, 32, 1024), F32),
             pltpu.VMEM((NBLK, N2, 256), F32),
             pltpu.VMEM((2, 2, N1, 128), F32),
-            pltpu.VMEM((16, 384, 128), F32),
+            pltpu.VMEM((16, 320, 128), F32),
             pltpu.VMEM((512, N2), BF),
-            pltpu.VMEM((256, N2), F32),
             pltpu.VMEM((BINS, 8, 128), F32),
             pltpu.VMEM((N2, 128), F32),
-            pltpu.SemaphoreType.DMA((11,)),
+            pltpu.VMEM((2, N2, 128), F32),
+            pltpu.VMEM((2, 64, 128), F32),
+            pltpu.SemaphoreType.DMA((8,)),
             pltpu.SemaphoreType.DMA((14,)),
             pltpu.SemaphoreType.DMA((8, 2)),
-            pltpu.SemaphoreType.DMA((5, 15)),
-            pltpu.SemaphoreType.DMA((5, 16)),
+            pltpu.SemaphoreType.DMA((9, 15)),
+            pltpu.SemaphoreType.DMA((9, 16)),
             pltpu.SemaphoreType.DMA((15,)),
             pltpu.SemaphoreType.DMA((15,)),
             pltpu.SemaphoreType.DMA,
@@ -524,10 +575,26 @@
     )(tmpl_pick, det_pick, edges, strain, tmpl, *tables)
 
 
-def snr_kernel(in_re, in_im, power, turn_c, turn_s, dft_hh, dft_l, out, stage_hl, order):
-    t = pl.program_id(0) // DET
+def snr_kernel(
+    own_series, in_re, in_im, power, total, turn_hbm, dft_hbm, out, turn, dft, stage_hl, order, sem
+):
+    i = pl.program_id(0)
+    pick = own_series[0]
+
+    @pl.when(i == 0)
+    def _():
+        copies = [
+            pltpu.make_async_copy(turn_hbm, turn, sem.at[0]),
+            pltpu.make_async_copy(dft_hbm, dft, sem.at[1]),
+        ]
+        for copy in copies:
+            copy.start()
+        for copy in copies:
+            copy.wait()
+
+    series = jnp.where(i == 5, pick, i + (i >= pick).astype(jnp.int32))
     _, owner = power_maps()
-    sigma_sq = jnp.sum(jnp.where(owner == t, sum_power(power), 0.0), keepdims=True)
+    sigma_sq = jnp.sum(jnp.where(owner == series // DET, sum_power(power), 0.0), keepdims=True)
     inv = 1.0 / jnp.sqrt(sigma_sq)
 
     def load(a, row):
@@ -535,87 +602,86 @@
         here = pl.ds(lax.rem(row, 32), 8)
         return in_re[source, here, :], in_im[source, here, :]
 
-    result = second_section(load, turn_c, turn_s, dft_hh, dft_l, stage_hl) * inv
-    for part in range(2):
-        for q in range(4):
-            order[pl.ds(q, 128, stride=4), :] = result[
-                part * 128 : part * 128 + 128, q * 128 : q * 128 + 128
-            ]
-        out[0, 0, part] = order[...].T
-
-
-def snr_of(arrived, power, turn, dft_hh, dft_l):
-    whole = lambda *shape: pl.BlockSpec(shape, lambda i: (0,) * len(shape))
+    def finish(result):
+        for part in range(2):
+            for q in range(4):
+                order[pl.ds(q, 128, stride=4), :] = (
+                    result[part * 128 : part * 128 + 128, q * 128 : q * 128 + 128] * inv
+                )
+            out[0, 0, part] = order[...].T
+
+    @pl.when(i < 5)
+    def _():
+        finish(second_section(load, turn, dft, stage_hl))
+
+    @pl.when(i == 5)
+    def _():
+        finish(total[...])
+
+
+def snr_of(own_series, arrived, power, total, turn, dft):
+    def out_map(i, pick):
+        series = jnp.where(i == 5, pick[0], i + (i >= pick[0]).astype(jnp.int32))
+        return series // DET, lax.rem(series, DET), 0, 0, 0
+
     return pl.pallas_call(
         snr_kernel,
         out_shape=jax.ShapeDtypeStruct((2, DET, 2, 128, N2), F32),
-        grid=(6,),
-        in_specs=[
-            pl.BlockSpec((16, 32, 128), lambda i: (0, i, 0)),
-            pl.BlockSpec((16, 32, 128), lambda i: (0, i + 6, 0)),
-            whole(16, 8, 128),
-            whole(3, 128, 128),
-            whole(3, 128, 128),
-            whole(256, 512),
-            whole(256, 256),
-        ],
-        out_specs=pl.BlockSpec((1, 1, 2, 128, N2), lambda i: (i // DET, lax.rem(i, DET), 0, 0, 0)),
-        scratch_shapes=[pltpu.VMEM((512, N2), BF), pltpu.VMEM((N2, 128), F32)],
-        compiler_params=pltpu.CompilerParams(vmem_limit_bytes=32 << 20),
+        grid_spec=pltpu.PrefetchScalarGridSpec(
+            num_scalar_prefetch=1,
+            grid=(6,),
+            in_specs=[
+                pl.BlockSpec((16, 32, 128), lambda i, pick: (0, jnp.minimum(i, 4), 0)),
+                pl.BlockSpec((16, 32, 128), lambda i, pick: (0, jnp.minimum(i, 4) + 5, 0)),
+                pl.BlockSpec((16, 8, 128), lambda i, pick: (0, 0, 0)),
+                pl.BlockSpec((256, N2), lambda i, pick: (0, 0)),
+                ANY,
+                ANY,
+            ],
+            out_specs=pl.BlockSpec((1, 1, 2, 128, N2), out_map),
+            scratch_shapes=[
+                pltpu.VMEM(turn.shape, F32),
+                pltpu.VMEM(dft.shape, BF),
+                pltpu.VMEM((512, N2), BF),
+                pltpu.VMEM((N2, 128), F32),
+                pltpu.SemaphoreType.DMA((2,)),
+            ],
+        ),
+        compiler_params=pltpu.CompilerParams(vmem_limit_bytes=60 << 20),
         name="snr",
-    )(arrived, arrived, power, *turn, dft_hh, dft_l)
-
-
-def turns(product, length):
-    angle = (product % length).astype(F32) * (2.0 * math.pi / length)
-    return jnp.cos(angle), jnp.sin(angle)
+    )(own_series, arrived, arrived, power, total, turn, dft)
 
 
 def fixed_turns(product, length):
     angle = 2.0 * np.pi * (product % length) / length
-    return np.cos(angle), np.sin(angle)
+    return np.stack([np.cos(angle), np.sin(angle)]).astype(np.float32)
 
 
 def fixed_tables():
     index = np.arange(128)
     c, s = fixed_turns(index[:, None] * index[None, :], 128)
-    full = np.concatenate(
-        [np.concatenate([c, -s], axis=1), np.concatenate([s, c], axis=1)], axis=0
-    ).astype(np.float32)
+    full = np.concatenate([np.concatenate([c, -s], axis=1), np.concatenate([s, c], axis=1)], axis=0)
     high = full.astype(jnp.bfloat16)
     low = (full - high.astype(np.float32)).astype(jnp.bfloat16)
-    spin = [
-        np.ascontiguousarray(np.broadcast_to(v[:, None, :], (16, 8, 128))).astype(np.float32)
-        for v in fixed_turns(np.arange(16)[:, None] * index[None, :], N1)
-    ]
-    turn = [
-        np.ascontiguousarray(np.broadcast_to(v[:, :, None], (3, 128, 128))).astype(np.float32)
-        for v in fixed_turns(np.arange(1, 4)[:, None] * index[None, :], N2)
-    ]
-    step = [
-        v.astype(np.float32)
-        for v in fixed_turns(np.arange(NBLK)[:, None] * index[None, :], NBLK)
-    ]
-    return high, low, spin, turn, step
+    dft = np.concatenate([high, high, low], axis=1)
+    spin = fixed_turns(np.arange(16)[:, None] * index[None, :], N1)
+    spin = np.ascontiguousarray(np.broadcast_to(spin[:, :, None, :], (2, 16, 8, 128)))
+    turn = fixed_turns(np.arange(1, 4)[:, None] * index[None, :], N2)
+    turn = np.ascontiguousarray(np.broadcast_to(turn[:, :, :, None], (2, 3, 128, 128)))
+    step = fixed_turns(np.arange(NBLK)[:, None] * index[None, :], NBLK)
+    factor = np.concatenate([np.arange(32), 4096 * np.arange(8), 512 * np.arange(8)])
+    fixed = fixed_turns(factor[:, None] * np.arange(N1)[None, :], N1 * N2)
+    rows = fixed_turns(32 * np.arange(16)[:, None] * np.arange(N1)[None, :], N1 * N2)
+    return spin, fixed, rows.reshape(2, 16, 16, 128), step, turn, dft
 
 
 def per_device(strain, templates, coinc_tmpl, coinc_det, bin_edges):
-    high, low, spin, turn, step = fixed_tables()
-    dft3 = np.concatenate([high, high, low], axis=1)
-    dft_hh = np.concatenate([high, high], axis=1)
-    place = lax.axis_index("freq")
-    rows = place * 32 + jnp.arange(32, dtype=jnp.int32)
-    times_all = jnp.arange(N1, dtype=jnp.int32)
-    times_own = place * 128 + jnp.arange(128, dtype=jnp.int32)
-    send_twist = turns(rows[:, None] * times_all[None, :], N1 * N2)
-    own_twist = turns(jnp.arange(N2, dtype=jnp.int32)[:, None] * times_own[None, :], N1 * N2)
-    base = turns(jnp.arange(64, dtype=jnp.int32)[:, None] * times_own[None, :], N1)
-    arrived, power_all, chi_sq = main_call(
+    spin, fixed, rows, step, turn, dft = fixed_tables()
+    arrived, power_all, total, chi_sq = main_call(
         coinc_tmpl, coinc_det, bin_edges, strain.reshape(2 * DET, 32, 256), templates,
-        np.stack(spin), jnp.stack(send_twist), jnp.stack(own_twist), jnp.stack(base),
-        np.stack(step), np.stack(turn), dft3, dft_hh, low,
+        spin, fixed, rows, step, turn, dft,
     )
-    snr = snr_of(arrived, power_all, turn, dft_hh, low)
+    snr = snr_of(DET * coinc_tmpl + coinc_det, arrived, power_all, total, turn, dft)
     return (snr, chi_sq)
 
 

time: 128 us -> 115 us (0.90)
  the two profiles are of different devices: /device:TPU:30 before, /device:TPU:102 now
where the time goes in v3:
time: 115 us
  Pallas kernels  112 us (97%)
  between operations  1.96 us (2%)
    pallas_call x1, Pallas kernels, main_call(): pl.pallas_call(main_kernel, out_shape=(jax.ShapeDtypeStruct((16, 320, 128...  103 us
    pallas_call x1, Pallas kernels, snr_of(): pl.pallas_call(snr_kernel, out_shape=jax.ShapeDtypeStruct((2, DET, 2, 128...  9.13 us

profile of v3, /device:TPU:102, one launch (start us, length us, event | category | flops | bytes accessed | tf_op | source)
XLA Modules:
  0.0 114.6 jit_solution(13907830024516888551)
XLA Ops:
  1.9 102.8 %main.1 = (f32[16,320,128]{2,1,0:T(8,128)}, f32[16,8,128]{2,1,0:T(8,128)}, f32[256,512]{1,0:T(8,128)}, f32[1,128,512]{2,1,0:T(8,128)}) custom-call(s32[1]{0:T(128)S(6)} %copy.14.tmpl_pick, s32[1]{0:T(128)S(6)} %copy.15.det_pick, s32[2,15]{1,0:T(2,128)} %edges.1, f32[6,32,256]{2,1,0:T(8,128)} %bitcast.1, f32[2,2,32,2048]{3,2,1,0:T(8,128)} %tmpl_hbm.1, ...), custom_call_target="tpu_custom_call" | custom-call | tf_op jit(solution)/shard_map/main/pallas_call | solution.py:541
  104.8 0.0 copy-start
  104.8 9.1 %snr.1 = f32[2,3,2,128,512]{4,3,2,1,0:T(8,128)} custom-call(s32[1]{0:T(128)S(6)} %add.3.own_series, f32[16,320,128]{2,1,0:T(8,128)} %get-tuple-element.6.in_re.in_im, f32[16,320,128]{2,1,0:T(8,128)} %get-tuple-element.6.in_re.in_im, f32[16,8,128]{2,1,0:T(8,128)} %get-tuple-element.7.power, f32[256,512]{1,0:T(8,128)} %get-tuple-element.8.total, ...), custom_call_target="tpu_custom_call" | custom-call | tf_op jit(solution)/shard_map/snr/pallas_call | solution.py:627
  113.9 0.0 copy-done
  113.9 0.7 copy.16
Async XLA Ops:
  104.8 9.2 %copy-start = (f32[1,128,512]{2,1,0:T(8,128)S(1)}, f32[1,128,512]{2,1,0:T(8,128)}, u32[]{:S(2)}) copy-start(f32[1,128,512]{2,1,0:T(8,128)} %get-tuple-element.13) | copy-start | bytes 786436

commit v4 on v3

--- a/solution.py
+++ b/solution.py
@@ -94,7 +94,8 @@
     arrived, power_all, total, chi_out,
     strain, tmpl, spin, fixed, row_turn, step, turn, dft,
     gathered, sections, turned, outgoing, stage_hl, weight_s, order, own_twist, base,
-    table_sem, bank_send, bank_recv, freq_send, freq_recv, all_send, all_recv, local,
+    held, table_sem, bank_send, bank_recv, freq_send, freq_recv,
+    first_send, first_recv, second_send, second_recv, local,
 ):
     here_b = lax.axis_index("bank")
     me = lax.axis_index("freq")
@@ -121,11 +122,10 @@
     barrier = pltpu.get_barrier_semaphore()
     for peer in (up, down, twin):
         pl.semaphore_signal(barrier, inc=1, device_id={"bank": peer}, device_id_type=MESH)
-    for k in range(1, 16):
-        pl.semaphore_signal(
-            barrier, inc=1, device_id={"freq": lax.rem(me + k, 16)}, device_id_type=MESH
-        )
-    pl.semaphore_wait(barrier, 18)
+    for k in range(1, 4):
+        for peer in (my * 4 + lax.rem(mx + k, 4), lax.rem(my + k, 4) * 4 + mx):
+            pl.semaphore_signal(barrier, inc=1, device_id={"freq": peer}, device_id_type=MESH)
+    pl.semaphore_wait(barrier, 9)
 
     bank_sent = []
 
@@ -221,26 +221,6 @@
         go(p, owner, second, -s)
 
     tables[0].wait()
-    col = lax.broadcasted_iota(jnp.int32, (128, 128), 1)
-    depth = lax.broadcasted_iota(jnp.int32, (128, 128), 0)
-    own_power = jnp.zeros((8, 128), F32)
-    for t in range(2):
-        for g in range(2):
-            sums = []
-            for a in range(8 * g, 8 * g + 8):
-                lanes = pl.ds(a * 128, 128)
-                hr, hi = tmpl[t, 0, :, lanes], tmpl[t, 1, :, lanes]
-                sums.append(jnp.sum(hr * hr + hi * hi, axis=0, keepdims=True))
-            select = (col == 4 * t + 2 * g + depth // 64).astype(F32)
-            own_power += jnp.dot(
-                jnp.concatenate(sums, axis=0),
-                select,
-                precision=lax.Precision.HIGHEST,
-                preferred_element_type=F32,
-            )
-    power_all[me] = own_power
-    begin(small)
-
     t_pick = tmpl_pick[0]
     d_pick = det_pick[0]
     own_series = DET * t_pick + d_pick
@@ -299,8 +279,6 @@
             landed(lax.rem(z + step_z, 4) * 2 + 1 - core, k)
         entry(quarters[i])
         both(begin, i)
-    both(near, 4)
-    both(other, 4)
     both(cross, 0, along=0)
     for k in range(2):
         landed(far, k)
@@ -309,6 +287,26 @@
         landed(lax.rem(z + 2, 4) * 2 + 1 - core, k)
     entry(quarters[3])
     both(begin, 3)
+    col = lax.broadcasted_iota(jnp.int32, (128, 128), 1)
+    depth = lax.broadcasted_iota(jnp.int32, (128, 128), 0)
+    own_power = jnp.zeros((8, 128), F32)
+    for t in range(2):
+        for g in range(2):
+            sums = []
+            for a in range(8 * g, 8 * g + 8):
+                lanes = pl.ds(a * 128, 128)
+                hr, hi = tmpl[t, 0, :, lanes], tmpl[t, 1, :, lanes]
+                sums.append(jnp.sum(hr * hr + hi * hi, axis=0, keepdims=True))
+            select = (col == 4 * t + 2 * g + depth // 64).astype(F32)
+            own_power += jnp.dot(
+                jnp.concatenate(sums, axis=0),
+                select,
+                precision=lax.Precision.HIGHEST,
+                preferred_element_type=F32,
+            )
+    power_all[me] = own_power
+
+    begin(small)
 
     tables[2].wait()
 
@@ -372,8 +370,9 @@
                     for before, after in zip(series[slot], series[slot + 1])
                 ]
                 out_re, out_im = times(value, c, s)
-                outgoing[f, 32 * slot : 32 * slot + 32, :] = out_re
-                outgoing[f, 160 + 32 * slot : 192 + 32 * slot, :] = out_im
+                rows = slice(32 * slot, 32 * slot + 32)
+                outgoing[0, lax.rem(f, 4), f // 4, rows, :] = out_re
+                outgoing[1, f // 4, lax.rem(f, 4), rows, :] = out_im
 
     for q in range(16):
         sections[q // 2, (q % 2) * 256 + 192 : (q % 2) * 256 + 256, :] = jnp.zeros((64, 256), F32)
@@ -381,16 +380,20 @@
     both(near, 1, 2)
     radix_steps(6, 12)
     both(other, 1, 2)
-    both(distant, 0, 4)
+    both(distant, 0)
+    both(near, 4)
+    both(other, 4)
+    radix_steps(12, 18)
+    both(cross, 0, along=-1)
     both(cross, 4, along=0)
-    radix_steps(12, 18)
-    both(cross, 0, 4, along=-1)
     radix_steps(18, 24)
     both(cross, 1, 2, along=0)
     both(near, 3)
     tables[3].wait()
     line_steps(0, 4)
     both(distant, 1, 2)
+    both(distant, 4)
+    both(cross, 4, along=-1)
     both(other, 3)
     line_steps(4, 8)
     both(cross, 0, 4, along=1)
@@ -432,26 +435,61 @@
         base[1, 8 * u : 8 * u + 8, :] = out_s
     both(cross, 3, along=2)
 
+    all_sent = []
+
+    def device(part, along, across):
+        return across * 4 + along if part == 0 else along * 4 + across
+
+    def first_phase(part, k):
+        along = lax.rem((mx, my)[part] + k, 4)
+        copy = pltpu.make_async_remote_copy(
+            src_ref=outgoing.at[part, along],
+            dst_ref=held.at[part, k - 1],
+            send_sem=first_send.at[part, k - 1],
+            recv_sem=first_recv.at[part, k - 1],
+            device_id={"freq": device(part, along, (my, mx)[part])},
+            device_id_type=MESH,
+        )
+        copy.start()
+        all_sent.append(copy)
+
+    keeps = []
+
+    def second_phase(part, k):
+        mine = (mx, my)[part]
+        across = (my, mx)[part]
+        if k == 0:
+            block = outgoing.at[part, mine]
+        else:
+            block = held.at[part, k - 1]
+            pltpu.make_async_copy(block, block, first_recv.at[part, k - 1]).wait()
+        target = arrived.at[part, device(part, lax.rem(mine + 4 - k, 4), across)]
+        for j in (2, 1, 3):
+            other_end = lax.rem(across + j, 4)
+            copy = pltpu.make_async_remote_copy(
+                src_ref=block.at[other_end],
+                dst_ref=target,
+                send_sem=second_send.at[part, k, j - 1],
+                recv_sem=second_recv.at[part, k, j - 1],
+                device_id={"freq": device(part, mine, other_end)},
+                device_id_type=MESH,
+            )
+            copy.start()
+            all_sent.append(copy)
+        keep = pltpu.make_async_copy(block.at[across], target, local.at[part, k])
+        keep.start()
+        keeps.append(keep)
+
     for along in (0, -1, 1, 2):
         for across in (1, 2):
             for p, (first, second, s) in enumerate(plans):
                 came(p, place(first, along * s, across * s))
 
-    keep = pltpu.make_async_copy(outgoing.at[me], arrived.at[me], local)
-    keep.start()
-    all_sent = []
-    for i, k in enumerate((10, 9, 11, 6, 14, 7, 13, 5, 15, 3, 8, 2, 12, 4, 1)):
-        peer = lax.rem(me + k, 16)
-        copy = pltpu.make_async_remote_copy(
-            src_ref=outgoing.at[peer],
-            dst_ref=arrived.at[me],
-            send_sem=all_send.at[k - 1],
-            recv_sem=all_recv.at[k - 1],
-            device_id={"freq": peer},
-            device_id_type=MESH,
-        )
-        copy.start()
-        all_sent.append(copy)
+    for k in (2, 1, 3):
+        for part in range(2):
+            first_phase(part, k)
+    for part in range(2):
+        second_phase(part, 0)
 
     for i in (5, 6):
         tables[i].wait()
@@ -488,20 +526,27 @@
 
     total[...] = jnp.zeros((256, N2), F32)
 
-    @pl.loop(0, BINS)
-    def _(level):
-        edge = edges[t_pick, jnp.minimum(level, BINS - 2)]
-        last = jnp.clip(jnp.where(level == BINS - 1, NBLK, edge) - 1, 0, NBLK - 1)
-
-        def load(a, row):
-            here = pl.ds(a * 128 + row, 8)
-            value = (sections[last, here, 0:128], sections[last, here, 128:256])
-            return times(value, own_twist[0, here, :], own_twist[1, here, :])
-
-        result = second_section(load, turn, dft, stage_hl)
-        sections[level, 0:256, :] = result[:, 0:256]
-        sections[level, 256:512, :] = result[:, 256:512]
-        total[...] += result
+    def bin_steps(start, stop):
+        @pl.loop(start, stop)
+        def _(level):
+            edge = edges[t_pick, jnp.minimum(level, BINS - 2)]
+            last = jnp.clip(jnp.where(level == BINS - 1, NBLK, edge) - 1, 0, NBLK - 1)
+
+            def load(a, row):
+                here = pl.ds(a * 128 + row, 8)
+                value = (sections[last, here, 0:128], sections[last, here, 128:256])
+                return times(value, own_twist[0, here, :], own_twist[1, here, :])
+
+            result = second_section(load, turn, dft, stage_hl)
+            sections[level, 0:256, :] = result[:, 0:256]
+            sections[level, 256:512, :] = result[:, 256:512]
+            total[...] += result
+
+    bin_steps(0, 6)
+    for k in (1, 3, 2):
+        for part in range(2):
+            second_phase(part, k)
+    bin_steps(6, BINS)
 
     inv = 1.0 / sigma_sq
 
@@ -524,10 +569,16 @@
 
     chi_out[0] = order[...].T
 
-    for k in range(1, 16):
-        source = lax.rem(me + 16 - k, 16)
-        pltpu.make_async_copy(arrived.at[source], arrived.at[source], all_recv.at[k - 1]).wait()
-    keep.wait()
+    for part in range(2):
+        for k in range(4):
+            for j in range(1, 4):
+                source = device(
+                    part, lax.rem((mx, my)[part] + 4 - k, 4), lax.rem((my, mx)[part] + 4 - j, 4)
+                )
+                block = arrived.at[part, source]
+                pltpu.make_async_copy(block, block, second_recv.at[part, k, j - 1]).wait()
+    for keep in keeps:
+        keep.wait()
     for copy in bank_sent + freq_sent + all_sent:
         copy.wait_send()
 
@@ -541,7 +592,7 @@
     return pl.pallas_call(
         main_kernel,
         out_shape=(
-            jax.ShapeDtypeStruct((16, 320, 128), F32),
+            jax.ShapeDtypeStruct((2, 16, 160, 128), F32),
             jax.ShapeDtypeStruct((16, 8, 128), F32),
             jax.ShapeDtypeStruct((256, N2), F32),
             jax.ShapeDtypeStruct((1, 128, N2), F32),
@@ -553,20 +604,23 @@
             pltpu.VMEM((16, 4, 32, 1024), F32),
             pltpu.VMEM((NBLK, N2, 256), F32),
             pltpu.VMEM((2, 2, N1, 128), F32),
-            pltpu.VMEM((16, 320, 128), F32),
+            pltpu.VMEM((2, 4, 4, 160, 128), F32),
             pltpu.VMEM((512, N2), BF),
             pltpu.VMEM((BINS, 8, 128), F32),
             pltpu.VMEM((N2, 128), F32),
             pltpu.VMEM((2, N2, 128), F32),
             pltpu.VMEM((2, 64, 128), F32),
+            pltpu.VMEM((2, 3, 4, 160, 128), F32),
             pltpu.SemaphoreType.DMA((8,)),
             pltpu.SemaphoreType.DMA((14,)),
             pltpu.SemaphoreType.DMA((8, 2)),
             pltpu.SemaphoreType.DMA((9, 15)),
             pltpu.SemaphoreType.DMA((9, 16)),
-            pltpu.SemaphoreType.DMA((15,)),
-            pltpu.SemaphoreType.DMA((15,)),
-            pltpu.SemaphoreType.DMA,
+            pltpu.SemaphoreType.DMA((2, 3)),
+            pltpu.SemaphoreType.DMA((2, 3)),
+            pltpu.SemaphoreType.DMA((2, 4, 3)),
+            pltpu.SemaphoreType.DMA((2, 4, 3)),
+            pltpu.SemaphoreType.DMA((2, 4)),
         ],
         compiler_params=pltpu.CompilerParams(
             collective_id=1, has_side_effects=True, vmem_limit_bytes=56 << 20
@@ -600,7 +654,7 @@
     def load(a, row):
         source = 4 * a + row // 32
         here = pl.ds(lax.rem(row, 32), 8)
-        return in_re[source, here, :], in_im[source, here, :]
+        return in_re[0, source, here, :], in_im[0, source, here, :]
 
     def finish(result):
         for part in range(2):
@@ -631,8 +685,8 @@
             num_scalar_prefetch=1,
             grid=(6,),
             in_specs=[
-                pl.BlockSpec((16, 32, 128), lambda i, pick: (0, jnp.minimum(i, 4), 0)),
-                pl.BlockSpec((16, 32, 128), lambda i, pick: (0, jnp.minimum(i, 4) + 5, 0)),
+                pl.BlockSpec((1, 16, 32, 128), lambda i, pick: (0, 0, jnp.minimum(i, 4), 0)),
+                pl.BlockSpec((1, 16, 32, 128), lambda i, pick: (1, 0, jnp.minimum(i, 4), 0)),
                 pl.BlockSpec((16, 8, 128), lambda i, pick: (0, 0, 0)),
                 pl.BlockSpec((256, N2), lambda i, pick: (0, 0)),
                 ANY,

time: 115 us -> 102 us (0.89)
  the two profiles are of different devices: /device:TPU:102 before, /device:TPU:0 now
where the time goes in v4:
time: 102 us; the launch traced here: 101 us
  Pallas kernels  98.3 us (96%)
  between operations  1.96 us (2%)
    pallas_call x1, Pallas kernels, main_call(): pl.pallas_call(main_kernel, out_shape=(jax.ShapeDtypeStruct((2, 16, 160,...  89.1 us
    pallas_call x1, Pallas kernels, snr_of(): pl.pallas_call(snr_kernel, out_shape=jax.ShapeDtypeStruct((2, DET, 2, 128...  9.12 us

profile of v4, /device:TPU:0, one launch (start us, length us, event | category | flops | bytes accessed | tf_op | source)
XLA Modules:
  0.0 100.9 jit_solution(10013674696810570672)
XLA Ops:
  1.9 89.1 %main.1 = (f32[2,16,160,128]{3,2,1,0:T(8,128)}, f32[16,8,128]{2,1,0:T(8,128)}, f32[256,512]{1,0:T(8,128)}, f32[1,128,512]{2,1,0:T(8,128)}) custom-call(s32[1]{0:T(128)S(6)} %copy.14.tmpl_pick, s32[1]{0:T(128)S(6)} %copy.15.det_pick, s32[2,15]{1,0:T(2,128)} %edges.1, f32[6,32,256]{2,1,0:T(8,128)} %bitcast.1, f32[2,2,32,2048]{3,2,1,0:T(8,128)} %tmpl_hbm.1, ...), custom_call_target="tpu_custom_call" | custom-call | tf_op jit(solution)/shard_map/main/pallas_call | solution.py:592
  91.1 0.0 copy-start
  91.1 9.1 %snr.1 = f32[2,3,2,128,512]{4,3,2,1,0:T(8,128)} custom-call(s32[1]{0:T(128)S(6)} %add.3.own_series, f32[2,16,160,128]{3,2,1,0:T(8,128)} %get-tuple-element.6.in_re.in_im, f32[2,16,160,128]{3,2,1,0:T(8,128)} %get-tuple-element.6.in_re.in_im, f32[16,8,128]{2,1,0:T(8,128)} %get-tuple-element.7.power, f32[256,512]{1,0:T(8,128)} %get-tuple-element.8.total, ...), custom_call_target="tpu_custom_call" | custom-call | tf_op jit(solution)/shard_map/snr/pallas_call | solution.py:681
  100.2 0.0 copy-done
  100.2 0.7 copy.16
Async XLA Ops:
  91.1 9.1 %copy-start = (f32[1,128,512]{2,1,0:T(8,128)S(1)}, f32[1,128,512]{2,1,0:T(8,128)}, u32[]{:S(2)}) copy-start(f32[1,128,512]{2,1,0:T(8,128)} %get-tuple-element.13) | copy-start | bytes 786436

commit v5 on v4

--- a/solution.py
+++ b/solution.py
@@ -91,9 +91,9 @@
 
 def main_kernel(
     tmpl_pick, det_pick, edges, strain_hbm, tmpl_hbm, spin_hbm, fixed_hbm, row_hbm, step_hbm, turn_hbm, dft_hbm,
-    arrived, power_all, total, chi_out,
+    arrived, power_all, total, order,
     strain, tmpl, spin, fixed, row_turn, step, turn, dft,
-    gathered, sections, turned, outgoing, stage_hl, weight_s, order, own_twist, base,
+    gathered, sections, turned, outgoing, stage_hl, weight_s, own_twist, base,
     held, table_sem, bank_send, bank_recv, freq_send, freq_recv,
     first_send, first_recv, second_send, second_recv, local,
 ):
@@ -160,14 +160,16 @@
 
     plans = [("x", "y", 1), ("y", "x", -1), ("x", "y", -1), ("y", "x", 1)] * 2 + [("x", "y", 1)]
     small = 8
-    quarters = [z, lax.rem(z + 1, 4), lax.rem(z + 3, 4), lax.rem(z + 2, 4)]
+    shards = [here_b, twin, up, down]
+    shards += [lax.rem(z + 1, 4) * 2 + 1 - core, lax.rem(z + 3, 4) * 2 + 1 - core]
+    shards += [far, lax.rem(z + 2, 4) * 2 + 1 - core]
     freq_sent = []
     counts = [0] * 9
 
     def part(p, owner):
         if p == small:
             return power_all.at[owner]
-        return gathered.at[owner, quarters[p // 2], pl.ds(16 * (p % 2), 16)]
+        return gathered.at[owner, shards[p]]
 
     def go(p, owner, axis, off):
         copy = pltpu.make_async_remote_copy(
@@ -226,29 +228,28 @@
     own_series = DET * t_pick + d_pick
     left = lax.broadcasted_iota(jnp.int32, (8, 128), 1) < 64
 
-    def entry(quarter):
+    def entry(shard):
         @pl.loop(0, 4)
         def _(chunk):
             rows = pl.ds(pl.multiple_of(chunk * 8, 8), 8)
-            for sub in range(4):
-                lanes = pl.ds(pl.multiple_of(quarter * 512 + sub * 128, 128), 128)
-                half = slice((sub % 2) * 128, (sub % 2) * 128 + 128)
-                who = quarter * 2 + sub // 2
+            for sub in range(2):
+                lanes = pl.ds(pl.multiple_of(shard * 256 + sub * 128, 128), 128)
+                half = slice(sub * 128, sub * 128 + 128)
                 hr, hi = tmpl[t_pick, 0, rows, lanes], tmpl[t_pick, 1, rows, lanes]
                 sr, si = [
                     jnp.where(
                         d_pick == 0,
-                        strain[who, k, rows, half],
+                        strain[shard, k, rows, half],
                         jnp.where(
-                            d_pick == 1, strain[who, 2 + k, rows, half], strain[who, 4 + k, rows, half]
+                            d_pick == 1, strain[shard, 2 + k, rows, half], strain[shard, 4 + k, rows, half]
                         ),
                     )
                     for k in range(2)
                 ]
                 re, im = hr * sr + hi * si, hr * si - hi * sr
                 re_far, im_far = pltpu.roll(re, 64, 1), pltpu.roll(im, 64, 1)
-                gathered[me, quarter, rows, 256 * sub : 256 * sub + 128] = jnp.where(left, re, im_far)
-                gathered[me, quarter, rows, 256 * sub + 128 : 256 * sub + 256] = jnp.where(
+                gathered[me, shard, rows, 256 * sub : 256 * sub + 128] = jnp.where(left, re, im_far)
+                gathered[me, shard, rows, 256 * sub + 128 : 256 * sub + 256] = jnp.where(
                     left, re_far, im
                 )
 
@@ -257,11 +258,15 @@
             for p in (small,) if i == 4 else (2 * i, 2 * i + 1):
                 act(p) if along is None else act(p, along)
 
+    def add_piece(p):
+        entry(shards[p])
+        begin(p)
+
     tables[1].wait()
+    add_piece(0)
     for k in range(2):
         landed(twin, k)
-    entry(quarters[0])
-    both(begin, 0)
+    add_piece(1)
     landed(down, 0)
     pass_on(down, 0, up)
     pass_on(down, 0, twin)
@@ -270,23 +275,24 @@
     pass_on(up, 1, twin)
     landed(up, 0)
     pass_on(up, 0, twin)
+    add_piece(2)
     landed(down, 1)
     pass_on(down, 1, twin)
+    add_piece(3)
     both(near, 0)
     both(other, 0)
-    for i, step_z in ((1, 1), (2, 3)):
+    for p in (4, 5):
         for k in range(2):
-            landed(lax.rem(z + step_z, 4) * 2 + 1 - core, k)
-        entry(quarters[i])
-        both(begin, i)
+            landed(shards[p], k)
+        add_piece(p)
     both(cross, 0, along=0)
     for k in range(2):
         landed(far, k)
         pass_on(far, k, twin)
+    add_piece(6)
     for k in range(2):
-        landed(lax.rem(z + 2, 4) * 2 + 1 - core, k)
-    entry(quarters[3])
-    both(begin, 3)
+        landed(shards[7], k)
+    add_piece(7)
     col = lax.broadcasted_iota(jnp.int32, (128, 128), 1)
     depth = lax.broadcasted_iota(jnp.int32, (128, 128), 0)
     own_power = jnp.zeros((8, 128), F32)
@@ -486,10 +492,10 @@
                 came(p, place(first, along * s, across * s))
 
     for k in (2, 1, 3):
-        for part in range(2):
-            first_phase(part, k)
-    for part in range(2):
-        second_phase(part, 0)
+        for side in range(2):
+            first_phase(side, k)
+    for side in range(2):
+        second_phase(side, 0)
 
     for i in (5, 6):
         tables[i].wait()
@@ -511,8 +517,8 @@
             [jnp.concatenate([wr, wi], axis=1), jnp.concatenate([-wi, wr], axis=1)], axis=0
         )
         m_high, m_low = split(matrix)
-        lanes = pl.ds(pl.multiple_of(lax.rem(b, 8) * 128, 128), 128)
-        high, low = split(gathered[:, b // 8, :, lanes].reshape(N2, 128))
+        lanes = pl.ds(pl.multiple_of(lax.rem(b, 4) * 128, 128), 128)
+        high, low = split(gathered[:, b // 4, :, lanes].reshape(N2, 128))
         section = jnp.dot(
             jnp.concatenate([high, low], axis=1),
             jnp.concatenate([m_high, m_high], axis=0),
@@ -567,8 +573,6 @@
                 sums += (dev_re * dev_re + dev_im * dev_im) * (1.0 / weight)
             order[pl.ds(q + 4 * row, 8, stride=4), :] = sums * inv
 
-    chi_out[0] = order[...].T
-
     for part in range(2):
         for k in range(4):
             for j in range(1, 4):
@@ -595,19 +599,18 @@
             jax.ShapeDtypeStruct((2, 16, 160, 128), F32),
             jax.ShapeDtypeStruct((16, 8, 128), F32),
             jax.ShapeDtypeStruct((256, N2), F32),
-            jax.ShapeDtypeStruct((1, 128, N2), F32),
+            jax.ShapeDtypeStruct((N2, 128), F32),
         ),
         in_specs=[SMEM] * 3 + [ANY] * (2 + len(tables)),
         out_specs=(ANY, vmem, vmem, vmem),
         scratch_shapes=shapes
         + [
-            pltpu.VMEM((16, 4, 32, 1024), F32),
+            pltpu.VMEM((16, 8, 32, 512), F32),
             pltpu.VMEM((NBLK, N2, 256), F32),
             pltpu.VMEM((2, 2, N1, 128), F32),
             pltpu.VMEM((2, 4, 4, 160, 128), F32),
             pltpu.VMEM((512, N2), BF),
             pltpu.VMEM((BINS, 8, 128), F32),
-            pltpu.VMEM((N2, 128), F32),
             pltpu.VMEM((2, N2, 128), F32),
             pltpu.VMEM((2, 64, 128), F32),
             pltpu.VMEM((2, 3, 4, 160, 128), F32),
@@ -630,22 +633,10 @@
 
 
 def snr_kernel(
-    own_series, in_re, in_im, power, total, turn_hbm, dft_hbm, out, turn, dft, stage_hl, order, sem
+    own_series, in_re, in_im, power, total, chi_in, turn, dft, out, chi_out, stage_hl, order
 ):
     i = pl.program_id(0)
     pick = own_series[0]
-
-    @pl.when(i == 0)
-    def _():
-        copies = [
-            pltpu.make_async_copy(turn_hbm, turn, sem.at[0]),
-            pltpu.make_async_copy(dft_hbm, dft, sem.at[1]),
-        ]
-        for copy in copies:
-            copy.start()
-        for copy in copies:
-            copy.wait()
-
     series = jnp.where(i == 5, pick, i + (i >= pick).astype(jnp.int32))
     _, owner = power_maps()
     sigma_sq = jnp.sum(jnp.where(owner == series // DET, sum_power(power), 0.0), keepdims=True)
@@ -671,16 +662,20 @@
     @pl.when(i == 5)
     def _():
         finish(total[...])
-
-
-def snr_of(own_series, arrived, power, total, turn, dft):
+        chi_out[0] = chi_in[...].T
+
+
+def snr_of(own_series, arrived, power, total, chi_in, turn, dft):
     def out_map(i, pick):
         series = jnp.where(i == 5, pick[0], i + (i >= pick[0]).astype(jnp.int32))
         return series // DET, lax.rem(series, DET), 0, 0, 0
 
     return pl.pallas_call(
         snr_kernel,
-        out_shape=jax.ShapeDtypeStruct((2, DET, 2, 128, N2), F32),
+        out_shape=(
+            jax.ShapeDtypeStruct((2, DET, 2, 128, N2), F32),
+            jax.ShapeDtypeStruct((1, 128, N2), F32),
+        ),
         grid_spec=pltpu.PrefetchScalarGridSpec(
             num_scalar_prefetch=1,
             grid=(6,),
@@ -689,21 +684,22 @@
                 pl.BlockSpec((1, 16, 32, 128), lambda i, pick: (1, 0, jnp.minimum(i, 4), 0)),
                 pl.BlockSpec((16, 8, 128), lambda i, pick: (0, 0, 0)),
                 pl.BlockSpec((256, N2), lambda i, pick: (0, 0)),
-                ANY,
-                ANY,
+                pl.BlockSpec((N2, 128), lambda i, pick: (0, 0)),
+                pl.BlockSpec(turn.shape, lambda i, pick: (0, 0, 0, 0)),
+                pl.BlockSpec(dft.shape, lambda i, pick: (0, 0)),
             ],
-            out_specs=pl.BlockSpec((1, 1, 2, 128, N2), out_map),
+            out_specs=(
+                pl.BlockSpec((1, 1, 2, 128, N2), out_map),
+                pl.BlockSpec((1, 128, N2), lambda i, pick: (0, 0, 0)),
+            ),
             scratch_shapes=[
-                pltpu.VMEM(turn.shape, F32),
-                pltpu.VMEM(dft.shape, BF),
                 pltpu.VMEM((512, N2), BF),
                 pltpu.VMEM((N2, 128), F32),
-                pltpu.SemaphoreType.DMA((2,)),
             ],
         ),
         compiler_params=pltpu.CompilerParams(vmem_limit_bytes=60 << 20),
         name="snr",
-    )(own_series, arrived, arrived, power, total, turn, dft)
+    )(own_series, arrived, arrived, power, total, chi_in, turn, dft)
 
 
 def fixed_turns(product, length):
@@ -731,12 +727,12 @@
 
 def per_device(strain, templates, coinc_tmpl, coinc_det, bin_edges):
     spin, fixed, rows, step, turn, dft = fixed_tables()
-    arrived, power_all, total, chi_sq = main_call(
+    arrived, power_all, total, chi_order = main_call(
         coinc_tmpl, coinc_det, bin_edges, strain.reshape(2 * DET, 32, 256), templates,
         spin, fixed, rows, step, turn, dft,
     )
-    snr = snr_of(DET * coinc_tmpl + coinc_det, arrived, power_all, total, turn, dft)
-    return (snr, chi_sq)
+    own_series = DET * coinc_tmpl + coinc_det
+    return snr_of(own_series, arrived, power_all, total, chi_order, turn, dft)
 
 
 def solution(mesh):

time: 102 us -> 99.4 us (0.975)
  Pallas kernels: 98.3 us -> 96.5 us
where the time goes in v5:
time: 99.4 us; the launch traced here: 98.5 us
  Pallas kernels  96.5 us (97%)
  between operations  1.93 us (2%)
    pallas_call x1, Pallas kernels, main_call(): pl.pallas_call(main_kernel, out_shape=(jax.ShapeDtypeStruct((2, 16, 160,...  88.2 us
    pallas_call x1, Pallas kernels, snr_of(): pl.pallas_call(snr_kernel, out_shape=(jax.ShapeDtypeStruct((2, DET, 2, 12...  8.39 us

profile of v5, /device:TPU:0, one launch (start us, length us, event | category | flops | bytes accessed | tf_op | source)
XLA Modules:
  0.0 98.5 jit_solution(4314104514751281297)
XLA Ops:
  1.9 88.2 %main.1 = (f32[2,16,160,128]{3,2,1,0:T(8,128)}, f32[16,8,128]{2,1,0:T(8,128)}, f32[256,512]{1,0:T(8,128)}, f32[512,128]{1,0:T(8,128)}) custom-call(s32[1]{0:T(128)S(6)} %copy.13.tmpl_pick, s32[1]{0:T(128)S(6)} %copy.14.det_pick, s32[2,15]{1,0:T(2,128)} %edges.1, f32[6,32,256]{2,1,0:T(8,128)} %bitcast.1, f32[2,2,32,2048]{3,2,1,0:T(8,128)} %tmpl_hbm.1, ...), custom_call_target="tpu_custom_call" | custom-call | tf_op jit(solution)/shard_map/main/pallas_call | solution.py:596
  90.1 8.4 %snr.1 = (f32[2,3,2,128,512]{4,3,2,1,0:T(8,128)}, f32[1,128,512]{2,1,0:T(8,128)}) custom-call(s32[1]{0:T(128)S(6)} %add.3.own_series, f32[2,16,160,128]{3,2,1,0:T(8,128)} %get-tuple-element.6.in_re.in_im, f32[2,16,160,128]{3,2,1,0:T(8,128)} %get-tuple-element.6.in_re.in_im, f32[16,8,128]{2,1,0:T(8,128)} %get-tuple-element.7.power, ...), custom_call_target="tpu_custom_call" | custom-call | tf_op jit(solution)/shard_map/snr/pallas_call | solution.py:673

commit v6 on v5

--- a/solution.py
+++ b/solution.py
@@ -91,11 +91,12 @@
 
 def main_kernel(
     tmpl_pick, det_pick, edges, strain_hbm, tmpl_hbm, spin_hbm, fixed_hbm, row_hbm, step_hbm, turn_hbm, dft_hbm,
-    arrived, power_all, total, order,
+    arrived, power_all, ready, order,
     strain, tmpl, spin, fixed, row_turn, step, turn, dft,
     gathered, sections, turned, outgoing, stage_hl, weight_s, own_twist, base,
+    total, early, staging, flip,
     held, table_sem, bank_send, bank_recv, freq_send, freq_recv,
-    first_send, first_recv, second_send, second_recv, local,
+    first_send, first_recv, second_send, second_recv, local, ready_sem,
 ):
     here_b = lax.axis_index("bank")
     me = lax.axis_index("freq")
@@ -446,57 +447,82 @@
     def device(part, along, across):
         return across * 4 + along if part == 0 else along * 4 + across
 
-    def first_phase(part, k):
+    waves = [pl.ds(0, 96), pl.ds(96, 64)]
+
+    def first_phase(part, k, wave):
         along = lax.rem((mx, my)[part] + k, 4)
         copy = pltpu.make_async_remote_copy(
-            src_ref=outgoing.at[part, along],
-            dst_ref=held.at[part, k - 1],
-            send_sem=first_send.at[part, k - 1],
-            recv_sem=first_recv.at[part, k - 1],
+            src_ref=outgoing.at[part, along, :, waves[wave]],
+            dst_ref=held.at[part, k - 1, :, waves[wave]],
+            send_sem=first_send.at[part, k - 1, wave],
+            recv_sem=first_recv.at[part, k - 1, wave],
             device_id={"freq": device(part, along, (my, mx)[part])},
             device_id_type=MESH,
         )
         copy.start()
         all_sent.append(copy)
 
-    keeps = []
-
-    def second_phase(part, k):
+    keeps = [[], []]
+
+    def landing(part, source, wave):
+        return arrived.at[part, source] if wave else early.at[part, source]
+
+    def second_phase(part, k, wave):
         mine = (mx, my)[part]
         across = (my, mx)[part]
         if k == 0:
-            block = outgoing.at[part, mine]
+            block = outgoing.at[part, mine, :, waves[wave]]
         else:
-            block = held.at[part, k - 1]
-            pltpu.make_async_copy(block, block, first_recv.at[part, k - 1]).wait()
-        target = arrived.at[part, device(part, lax.rem(mine + 4 - k, 4), across)]
+            block = held.at[part, k - 1, :, waves[wave]]
+            pltpu.make_async_copy(block, block, first_recv.at[part, k - 1, wave]).wait()
+        target = landing(part, device(part, lax.rem(mine + 4 - k, 4), across), wave)
         for j in (2, 1, 3):
             other_end = lax.rem(across + j, 4)
             copy = pltpu.make_async_remote_copy(
                 src_ref=block.at[other_end],
                 dst_ref=target,
-                send_sem=second_send.at[part, k, j - 1],
-                recv_sem=second_recv.at[part, k, j - 1],
+                send_sem=second_send.at[part, k, j - 1, wave],
+                recv_sem=second_recv.at[part, k, j - 1, wave],
                 device_id={"freq": device(part, mine, other_end)},
                 device_id_type=MESH,
             )
             copy.start()
             all_sent.append(copy)
-        keep = pltpu.make_async_copy(block.at[across], target, local.at[part, k])
+        keep = pltpu.make_async_copy(block.at[across], target, local.at[part, k, wave])
         keep.start()
-        keeps.append(keep)
+        keeps[wave].append(keep)
+
+    def open_wave(wave):
+        for k in (2, 1, 3):
+            for side in range(2):
+                first_phase(side, k, wave)
+        for side in range(2):
+            second_phase(side, 0, wave)
+
+    def forward_wave(wave):
+        for k in (1, 3, 2):
+            for side in range(2):
+                second_phase(side, k, wave)
+
+    def finish_wave(wave):
+        for side in range(2):
+            for k in range(4):
+                for j in range(1, 4):
+                    source = device(
+                        side, lax.rem((mx, my)[side] + 4 - k, 4), lax.rem((my, mx)[side] + 4 - j, 4)
+                    )
+                    block = landing(side, source, wave)
+                    pltpu.make_async_copy(block, block, second_recv.at[side, k, j - 1, wave]).wait()
+        for keep in keeps[wave]:
+            keep.wait()
 
     for along in (0, -1, 1, 2):
         for across in (1, 2):
             for p, (first, second, s) in enumerate(plans):
                 came(p, place(first, along * s, across * s))
 
-    for k in (2, 1, 3):
-        for side in range(2):
-            first_phase(side, k)
-    for side in range(2):
-        second_phase(side, 0)
-
+    open_wave(0)
+    open_wave(1)
     for i in (5, 6):
         tables[i].wait()
     block, owner = power_maps()
@@ -548,11 +574,11 @@
             sections[level, 256:512, :] = result[:, 256:512]
             total[...] += result
 
-    bin_steps(0, 6)
-    for k in (1, 3, 2):
-        for part in range(2):
-            second_phase(part, k)
-    bin_steps(6, BINS)
+    bin_steps(0, 10)
+    forward_wave(0)
+    bin_steps(10, 16)
+    forward_wave(1)
+    bin_steps(16, BINS)
 
     inv = 1.0 / sigma_sq
 
@@ -573,16 +599,43 @@
                 sums += (dev_re * dev_re + dev_im * dev_im) * (1.0 / weight)
             order[pl.ds(q + 4 * row, 8, stride=4), :] = sums * inv
 
-    for part in range(2):
-        for k in range(4):
-            for j in range(1, 4):
-                source = device(
-                    part, lax.rem((mx, my)[part] + 4 - k, 4), lax.rem((my, mx)[part] + 4 - j, 4)
+    sums = sum_power(power_all)
+    inv_sigma = [
+        1.0 / jnp.sqrt(jnp.sum(jnp.where(owner == t, sums, 0.0), keepdims=True)) for t in range(2)
+    ]
+
+    def emit(slot, series, result):
+        scale = jnp.where(series < DET, inv_sigma[0], inv_sigma[1])
+        for part in range(2):
+            for q in range(4):
+                flip[pl.ds(q, 128, stride=4), :] = (
+                    result[part * 128 : part * 128 + 128, q * 128 : q * 128 + 128] * scale
                 )
-                block = arrived.at[part, source]
-                pltpu.make_async_copy(block, block, second_recv.at[part, k, j - 1]).wait()
-    for keep in keeps:
-        keep.wait()
+            staging[slot, part] = flip[...].T
+
+    out_copies = [
+        pltpu.make_async_copy(staging.at[slot], ready.at[slot], ready_sem.at[slot])
+        for slot in range(4)
+    ]
+    emit(3, own_series, total[...])
+    out_copies[3].start()
+    finish_wave(0)
+
+    @pl.loop(0, 3)
+    def _(slot):
+        def load(a, row):
+            source = 4 * a + row // 32
+            here = pl.ds(pl.multiple_of(slot * 32 + lax.rem(row, 32), 8), 8)
+            return early[0, source, here, :], early[1, source, here, :]
+
+        series = slot + jnp.where(own_series <= slot, 1, 0)
+        emit(slot, series, second_section(load, turn, dft, stage_hl))
+
+    for slot in range(3):
+        out_copies[slot].start()
+    finish_wave(1)
+    for copy in out_copies:
+        copy.wait()
     for copy in bank_sent + freq_sent + all_sent:
         copy.wait_send()
 
@@ -596,13 +649,13 @@
     return pl.pallas_call(
         main_kernel,
         out_shape=(
-            jax.ShapeDtypeStruct((2, 16, 160, 128), F32),
+            jax.ShapeDtypeStruct((2, 16, 64, 128), F32),
             jax.ShapeDtypeStruct((16, 8, 128), F32),
-            jax.ShapeDtypeStruct((256, N2), F32),
+            jax.ShapeDtypeStruct((4, 2, 128, N2), F32),
             jax.ShapeDtypeStruct((N2, 128), F32),
         ),
         in_specs=[SMEM] * 3 + [ANY] * (2 + len(tables)),
-        out_specs=(ANY, vmem, vmem, vmem),
+        out_specs=(ANY, vmem, ANY, vmem),
         scratch_shapes=shapes
         + [
             pltpu.VMEM((16, 8, 32, 512), F32),
@@ -613,17 +666,22 @@
             pltpu.VMEM((BINS, 8, 128), F32),
             pltpu.VMEM((2, N2, 128), F32),
             pltpu.VMEM((2, 64, 128), F32),
+            pltpu.VMEM((256, N2), F32),
+            pltpu.VMEM((2, 16, 96, 128), F32),
+            pltpu.VMEM((4, 2, 128, N2), F32),
+            pltpu.VMEM((N2, 128), F32),
             pltpu.VMEM((2, 3, 4, 160, 128), F32),
             pltpu.SemaphoreType.DMA((8,)),
             pltpu.SemaphoreType.DMA((14,)),
             pltpu.SemaphoreType.DMA((8, 2)),
             pltpu.SemaphoreType.DMA((9, 15)),
             pltpu.SemaphoreType.DMA((9, 16)),
-            pltpu.SemaphoreType.DMA((2, 3)),
-            pltpu.SemaphoreType.DMA((2, 3)),
-            pltpu.SemaphoreType.DMA((2, 4, 3)),
-            pltpu.SemaphoreType.DMA((2, 4, 3)),
-            pltpu.SemaphoreType.DMA((2, 4)),
+            pltpu.SemaphoreType.DMA((2, 3, 2)),
+            pltpu.SemaphoreType.DMA((2, 3, 2)),
+            pltpu.SemaphoreType.DMA((2, 4, 3, 2)),
+            pltpu.SemaphoreType.DMA((2, 4, 3, 2)),
+            pltpu.SemaphoreType.DMA((2, 4, 2)),
+            pltpu.SemaphoreType.DMA((4,)),
         ],
         compiler_params=pltpu.CompilerParams(
             collective_id=1, has_side_effects=True, vmem_limit_bytes=56 << 20
@@ -633,11 +691,30 @@
 
 
 def snr_kernel(
-    own_series, in_re, in_im, power, total, chi_in, turn, dft, out, chi_out, stage_hl, order
+    own_series, arrived, power, chi_in, turn, dft, ready, out, chi_out, stage_hl, order, result, moved, sem
 ):
     i = pl.program_id(0)
     pick = own_series[0]
-    series = jnp.where(i == 5, pick, i + (i >= pick).astype(jnp.int32))
+
+    def spot(series):
+        return out.at[series // DET, lax.rem(series, DET)]
+
+    places = [slot + (slot >= pick).astype(jnp.int32) for slot in range(3)] + [pick]
+
+    def fetch(k):
+        return pltpu.make_async_copy(ready.at[k], moved.at[k], sem.at[k])
+
+    def store(k):
+        return pltpu.make_async_copy(moved.at[k], spot(places[k]), sem.at[6 + k])
+
+    @pl.when(i == 0)
+    def _():
+        for k in range(4):
+            fetch(k).start()
+        chi_out[0] = chi_in[...].T
+
+    slot = 3 + i
+    series = slot + (slot >= pick).astype(jnp.int32)
     _, owner = power_maps()
     sigma_sq = jnp.sum(jnp.where(owner == series // DET, sum_power(power), 0.0), keepdims=True)
     inv = 1.0 / jnp.sqrt(sigma_sq)
@@ -645,30 +722,35 @@
     def load(a, row):
         source = 4 * a + row // 32
         here = pl.ds(lax.rem(row, 32), 8)
-        return in_re[0, source, here, :], in_im[0, source, here, :]
-
-    def finish(result):
-        for part in range(2):
-            for q in range(4):
-                order[pl.ds(q, 128, stride=4), :] = (
-                    result[part * 128 : part * 128 + 128, q * 128 : q * 128 + 128] * inv
-                )
-            out[0, 0, part] = order[...].T
-
-    @pl.when(i < 5)
+        return arrived[0, source, here, :], arrived[1, source, here, :]
+
+    value = second_section(load, turn, dft, stage_hl)
+    for part in range(2):
+        for q in range(4):
+            order[pl.ds(q, 128, stride=4), :] = (
+                value[part * 128 : part * 128 + 128, q * 128 : q * 128 + 128] * inv
+            )
+        result[i, part] = order[...].T
+    pltpu.make_async_copy(result.at[i], spot(series), sem.at[4 + i]).start()
+
+    @pl.when(i == 0)
     def _():
-        finish(second_section(load, turn, dft, stage_hl))
-
-    @pl.when(i == 5)
+        for k in range(4):
+            fetch(k).wait()
+            store(k).start()
+
+    @pl.when(i == 1)
     def _():
-        finish(total[...])
-        chi_out[0] = chi_in[...].T
-
-
-def snr_of(own_series, arrived, power, total, chi_in, turn, dft):
-    def out_map(i, pick):
-        series = jnp.where(i == 5, pick[0], i + (i >= pick[0]).astype(jnp.int32))
-        return series // DET, lax.rem(series, DET), 0, 0, 0
+        for k in range(4):
+            store(k).wait()
+        for k in range(2):
+            last = 3 + k + (3 + k >= pick).astype(jnp.int32)
+            pltpu.make_async_copy(result.at[k], spot(last), sem.at[4 + k]).wait()
+
+
+def snr_of(own_series, arrived, power, ready, chi_in, turn, dft):
+    def whole(shape):
+        return pl.BlockSpec(shape, lambda i, pick: (0,) * len(shape))
 
     return pl.pallas_call(
         snr_kernel,
@@ -678,28 +760,27 @@
         ),
         grid_spec=pltpu.PrefetchScalarGridSpec(
             num_scalar_prefetch=1,
-            grid=(6,),
+            grid=(2,),
             in_specs=[
-                pl.BlockSpec((1, 16, 32, 128), lambda i, pick: (0, 0, jnp.minimum(i, 4), 0)),
-                pl.BlockSpec((1, 16, 32, 128), lambda i, pick: (1, 0, jnp.minimum(i, 4), 0)),
-                pl.BlockSpec((16, 8, 128), lambda i, pick: (0, 0, 0)),
-                pl.BlockSpec((256, N2), lambda i, pick: (0, 0)),
-                pl.BlockSpec((N2, 128), lambda i, pick: (0, 0)),
-                pl.BlockSpec(turn.shape, lambda i, pick: (0, 0, 0, 0)),
-                pl.BlockSpec(dft.shape, lambda i, pick: (0, 0)),
+                pl.BlockSpec((2, 16, 32, 128), lambda i, pick: (0, 0, i, 0)),
+                whole((16, 8, 128)),
+                whole((N2, 128)),
+                whole(turn.shape),
+                whole(dft.shape),
+                ANY,
             ],
-            out_specs=(
-                pl.BlockSpec((1, 1, 2, 128, N2), out_map),
-                pl.BlockSpec((1, 128, N2), lambda i, pick: (0, 0, 0)),
-            ),
+            out_specs=(ANY, whole((1, 128, N2))),
             scratch_shapes=[
                 pltpu.VMEM((512, N2), BF),
                 pltpu.VMEM((N2, 128), F32),
+                pltpu.VMEM((2, 2, 128, N2), F32),
+                pltpu.VMEM((4, 2, 128, N2), F32),
+                pltpu.SemaphoreType.DMA((10,)),
             ],
         ),
         compiler_params=pltpu.CompilerParams(vmem_limit_bytes=60 << 20),
         name="snr",
-    )(own_series, arrived, arrived, power, total, chi_in, turn, dft)
+    )(own_series, arrived, power, chi_in, turn, dft, ready)
 
 
 def fixed_turns(product, length):
@@ -727,12 +808,12 @@
 
 def per_device(strain, templates, coinc_tmpl, coinc_det, bin_edges):
     spin, fixed, rows, step, turn, dft = fixed_tables()
-    arrived, power_all, total, chi_order = main_call(
+    arrived, power_all, ready, chi_order = main_call(
         coinc_tmpl, coinc_det, bin_edges, strain.reshape(2 * DET, 32, 256), templates,
         spin, fixed, rows, step, turn, dft,
     )
     own_series = DET * coinc_tmpl + coinc_det
-    return snr_of(own_series, arrived, power_all, total, chi_order, turn, dft)
+    return snr_of(own_series, arrived, power_all, ready, chi_order, turn, dft)
 
 
 def solution(mesh):

time: 99.4 us -> 97.9 us (0.985)
    pallas_call x1, Pallas kernels: 8.39 us -> 5.5 us  [snr_of(): pl.pallas_call(snr_kernel, out_shape=(jax.ShapeDtypeStruct((2, DET, 2, 12...]
    pallas_call x1, Pallas kernels: 88.2 us -> 90.3 us  [main_call(): pl.pallas_call(main_kernel, out_shape=(jax.ShapeDtypeStruct((2, 16, 64, 1...]
where the time goes in v6:
time: 97.9 us; the launch traced here: 97.7 us
  Pallas kernels  95.8 us (98%)
  between operations  1.93 us (2%)
    pallas_call x1, Pallas kernels, main_call(): pl.pallas_call(main_kernel, out_shape=(jax.ShapeDtypeStruct((2, 16, 64, 1...  90.3 us
    pallas_call x1, Pallas kernels, snr_of(): pl.pallas_call(snr_kernel, out_shape=(jax.ShapeDtypeStruct((2, DET, 2, 12...  5.5 us

profile of v6, /device:TPU:0, one launch (start us, length us, event | category | flops | bytes accessed | tf_op | source)
XLA Modules:
  0.0 97.7 jit_solution(17513169207116967397)
XLA Ops:
  1.9 90.3 %main.1 = (f32[2,16,64,128]{3,2,1,0:T(8,128)}, f32[16,8,128]{2,1,0:T(8,128)}, f32[4,2,128,512]{3,2,1,0:T(8,128)}, f32[512,128]{1,0:T(8,128)}) custom-call(s32[1]{0:T(128)S(6)} %copy.13.tmpl_pick, s32[1]{0:T(128)S(6)} %copy.14.det_pick, s32[2,15]{1,0:T(2,128)} %edges.1, f32[6,32,256]{2,1,0:T(8,128)} %bitcast.1, f32[2,2,32,2048]{3,2,1,0:T(8,128)} %tmpl_hbm.1, ...), custom_call_target="tpu_custom_call" | custom-call | tf_op jit(solution)/shard_map/main/pallas_call | solution.py:649
  92.2 5.5 %snr.1 = (f32[2,3,2,128,512]{4,3,2,1,0:T(8,128)}, f32[1,128,512]{2,1,0:T(8,128)}) custom-call(s32[1]{0:T(128)S(6)} %add.3.own_series, f32[2,16,64,128]{3,2,1,0:T(8,128)} %get-tuple-element.6.arrived, f32[16,8,128]{2,1,0:T(8,128)} %get-tuple-element.7.power, f32[512,128]{1,0:T(8,128)} %get-tuple-element.8.chi_in, ...), custom_call_target="tpu_custom_call" | custom-call | tf_op jit(solution)/shard_map/snr/pallas_call | solution.py:755

commit v7 on v6

--- a/solution.py
+++ b/solution.py
@@ -496,8 +496,6 @@
         for k in (2, 1, 3):
             for side in range(2):
                 first_phase(side, k, wave)
-        for side in range(2):
-            second_phase(side, 0, wave)
 
     def forward_wave(wave):
         for k in (1, 3, 2):
@@ -523,6 +521,10 @@
 
     open_wave(0)
     open_wave(1)
+    for side in range(2):
+        second_phase(side, 0, 0)
+    for side in range(2):
+        second_phase(side, 0, 1)
     for i in (5, 6):
         tables[i].wait()
     block, owner = power_maps()

time: 97.9 us -> 97.9 us (level)
  no operation moved by 1% of the time
where the time goes in v7:
time: 97.9 us; the launch traced here: 97.7 us
  Pallas kernels  95.8 us (98%)
  between operations  1.93 us (2%)
    pallas_call x1, Pallas kernels, main_call(): pl.pallas_call(main_kernel, out_shape=(jax.ShapeDtypeStruct((2, 16, 64, 1...  90.3 us
    pallas_call x1, Pallas kernels, snr_of(): pl.pallas_call(snr_kernel, out_shape=(jax.ShapeDtypeStruct((2, DET, 2, 12...  5.5 us

profile of v7, /device:TPU:0, one launch (start us, length us, event | category | flops | bytes accessed | tf_op | source)
XLA Modules:
  0.0 97.7 jit_solution(7026292799304375143)
XLA Ops:
  1.9 90.3 %main.1 = (f32[2,16,64,128]{3,2,1,0:T(8,128)}, f32[16,8,128]{2,1,0:T(8,128)}, f32[4,2,128,512]{3,2,1,0:T(8,128)}, f32[512,128]{1,0:T(8,128)}) custom-call(s32[1]{0:T(128)S(6)} %copy.13.tmpl_pick, s32[1]{0:T(128)S(6)} %copy.14.det_pick, s32[2,15]{1,0:T(2,128)} %edges.1, f32[6,32,256]{2,1,0:T(8,128)} %bitcast.1, f32[2,2,32,2048]{3,2,1,0:T(8,128)} %tmpl_hbm.1, ...), custom_call_target="tpu_custom_call" | custom-call | tf_op jit(solution)/shard_map/main/pallas_call | solution.py:651
  92.2 5.5 %snr.1 = (f32[2,3,2,128,512]{4,3,2,1,0:T(8,128)}, f32[1,128,512]{2,1,0:T(8,128)}) custom-call(s32[1]{0:T(128)S(6)} %add.3.own_series, f32[2,16,64,128]{3,2,1,0:T(8,128)} %get-tuple-element.6.arrived, f32[16,8,128]{2,1,0:T(8,128)} %get-tuple-element.7.power, f32[512,128]{1,0:T(8,128)} %get-tuple-element.8.chi_in, ...), custom_call_target="tpu_custom_call" | custom-call | tf_op jit(solution)/shard_map/snr/pallas_call | solution.py:757
